TPU v7x, 512 devices: a whole 4x4x16 slice. The times are simulated.
512 devices in a mesh: wa: 4 (over x), vert: 128 (over y, z, core).
Axes of the slice: x: 4, y: 4, z: 16, core: 2. Of those that a mesh axis runs over, the one named last changes fastest.
Arguments:
- hidden: bfloat16 [16384, 1024], P('vert', 'wa'), as said below
- norm_gain: bfloat16 [1024], P('wa'), may hold values from 0.5 to 1.5
- head_weight: bfloat16 [1024, 32128], P('wa', 'vert'), as said below
- target_ids: int32 [16384], P('vert'), may hold values from 0 to 32127
- seq_lengths: int32 [65], replicated, may hold values from 1 to 8192, as said below
Outputs:
- token_logprob: float32 [16384], P('vert')
- token_entropy: float32 [16384], P('vert')
Inputs may be any that keep to these rules, and one draw needn't show every extreme that they name: `seq_lengths`: entry 0 equals 8192; every other entry lies between 1 and 128, and at least one of them equals 128. `hidden`: hidden states of any scale per slot; the norm removes it. `head_weight`: entries of order 3 / sqrt(1024) times a per-column scale.
All inputs are finite; a program needn't handle non-finite values.
Results may differ from a plain program's by a relative error of at most 0.012.
The roundings to bfloat16 on the way count: a program that leaves them out, or rounds other values in their place, can miss the bound.
Values may be sent and summed in bfloat16 or wider, within the bound.
A program may use at most 64 MiB of HBM per device.

v0:
```python
import jax
import jax.numpy as jnp
from jax import lax
from jax.sharding import Mesh
from jax.sharding import PartitionSpec as P

D = 1024
SHORT = 128


norm_epsilon = 1e-06

VERT = ("y", "z", "c")
TOKEN_AXES = ("z", "c")


def live_mask(positions, seq_lengths, long_len, short_len):
    is_long = positions < long_len
    beyond = jnp.maximum(positions - long_len, 0)
    seq_index = jnp.where(is_long, 0, 1 + beyond // short_len)
    offset = jnp.where(is_long, positions, beyond % short_len)
    return offset < jnp.take(seq_lengths, seq_index)


def per_device(hidden, norm_gain, head_weight, target_ids, seq_lengths):
    x_count = lax.axis_size("x")
    y_count = lax.axis_size("y")
    z_count = lax.axis_size("z")
    c_count = lax.axis_size("c")
    x_index = lax.axis_index("x")
    y_index = lax.axis_index("y")
    z_index = lax.axis_index("z")
    c_index = lax.axis_index("c")
    vert_count = y_count * z_count * c_count
    vert_index = (y_index * z_count + z_index) * c_count + c_index
    tok_local = hidden.shape[0]
    quarter = tok_local // x_count
    vocab_local = head_weight.shape[1]
    group_count = z_count * c_count

    rows = lax.all_to_all(hidden, "x", split_axis=0, concat_axis=1, tiled=True)
    gain_full = lax.all_gather(norm_gain, "x", axis=0, tiled=True)
    values = rows.astype(jnp.float32)
    squares = jnp.sum(values * values, axis=1, keepdims=True)
    normed = (
        values * lax.rsqrt(squares / D + norm_epsilon) * gain_full.astype(jnp.float32)
    ).astype(jnp.bfloat16)

    group_rows = lax.all_gather(normed, TOKEN_AXES, axis=0, tiled=True)
    group_ids = lax.all_gather(target_ids, TOKEN_AXES, axis=0)
    group_ids = lax.dynamic_slice_in_dim(group_ids, x_index * quarter, quarter, 1).reshape(-1)

    weight = lax.all_gather(head_weight, ("x", "y"), axis=0)
    weight = weight.reshape(x_count, y_count, D // x_count, vocab_local)
    logits = jnp.einsum(
        "txd,xyde->tye",
        group_rows.reshape(-1, x_count, D // x_count),
        weight,
        preferred_element_type=jnp.float32,
    )
    block_of = (lax.broadcasted_iota(jnp.int32, (1, y_count, vocab_local), 1) * z_count + z_index) * c_count + c_index
    column_ids = block_of * vocab_local + lax.broadcasted_iota(jnp.int32, (1, y_count, vocab_local), 2)
    row_peak = jnp.max(logits, axis=(1, 2))
    scaled = jnp.exp(logits - row_peak[:, None, None])
    row_sum = jnp.sum(scaled, axis=(1, 2))
    row_weighted = jnp.sum(scaled * logits, axis=(1, 2))
    row_picked = jnp.sum(jnp.where(column_ids == group_ids[:, None, None], logits, 0.0), axis=(1, 2))
    stats = jnp.stack([row_peak, row_sum, row_weighted, row_picked]).reshape(4, group_count, quarter)

    parts = lax.all_to_all(stats, TOKEN_AXES, split_axis=1, concat_axis=1, tiled=True)
    part_peak, part_sum, part_weighted, part_picked = parts[0], parts[1], parts[2], parts[3]
    highest = jnp.max(part_peak, axis=0)
    factor = jnp.exp(part_peak - highest[None, :])
    totals = jnp.sum(part_sum * factor, axis=0)
    weighted = jnp.sum(part_weighted * factor, axis=0)
    picked = jnp.sum(part_picked, axis=0)
    log_norm = highest + jnp.log(totals)
    logprob = picked - log_norm
    entropy = log_norm - weighted / totals
    full_logprob, full_entropy = (
        lax.all_gather(logprob, "x", axis=0, tiled=True),
        lax.all_gather(entropy, "x", axis=0, tiled=True),
    )
    positions = vert_index * tok_local + jnp.arange(tok_local, dtype=jnp.int32)
    live_rows = live_mask(positions, seq_lengths, vert_count * tok_local // 2, SHORT)
    return (jnp.where(live_rows, full_logprob, 0.0), jnp.where(live_rows, full_entropy, 0.0))


def solution(mesh):
    wa_count, vert_count = mesh.devices.shape
    y_count = 4
    c_count = 2
    z_count = vert_count // (y_count * c_count)
    fine = Mesh(mesh.devices.reshape(wa_count, y_count, z_count, c_count), ("x",) + VERT)
    in_specs = (P(VERT, "x"), P("x"), P("x", VERT), P(VERT), P())
    out_specs = (P(VERT), P(VERT))
    return jax.shard_map(
        per_device, mesh=fine, in_specs=in_specs, out_specs=out_specs, check_vma=False
    )
```

profile of v0, /device:TPU:24, one launch (start us, length us, event | category | flops | bytes accessed | tf_op | source)
XLA Modules:
  0.0 210.1 jit_solution(2471399766707559232)
XLA Ops:
  7.2 0.0 copy-start
  7.2 4.3 %all-to-all-start = ((bf16[4,32,256]{2,1,0:T(8,128)(2,1)}), bf16[4,32,256]{2,1,0:T(8,128)(2,1)S(1)}, u32[]{:S(2)}, u32[]{:S(2)}) async-start(bf16[4,32,256]{2,1,0:T(8,128)(2,1)} %bitcast.53), calls=%async_computation | async-start | bytes 131072 | tf_op jit(solution)/shard_map/all_to_all | solution.py:41
  11.5 0.0 all-gather.7.cloned.1.call-start
  11.5 0.7 reshape.134
  12.1 10.2 %all-gather.2 = bf16[4,1,256]{2,1,0:T(2,128)(2,1)S(1)} all-gather(bf16[1,1,256]{2,1,0:T(2,128)(2,1)S(1)} %reshape.134), channel_id=1, replica_groups=mesh['x'=4,'y'=4,'z'=16,'c'=2] {'x'}, dimensions={0}, use_global_device_ids=true | all-gather | bytes 2560 | tf_op jit(solution)/shard_map/all_gather | solution.py:42
  22.3 0.0 all-to-all-done
  22.4 0.1 fusion.4
  22.5 0.7 multiply_convert_fusion
  23.2 0.0 all-gather.7.cloned.1.call-update
  23.2 0.0 all-gather.9.cloned.1.call-start
  23.3 0.7 all-gather.9.cloned.1.call-update
  24.0 36.2 %all-gather.3 = s32[32,1,128]{2,1,0:T(1,128)S(1)} all-gather(s32[1,1,128]{2,1,0:T(1,128)} %bitcast.55), channel_id=3, replica_groups=mesh['x'=4,'y'=4,'z'=16,'c'=2] {'z','c'}, dimensions={0}, use_global_device_ids=true | all-gather | bytes 16896 | tf_op jit(solution)/shard_map/all_gather | solution.py:50
  60.2 0.1 dynamic-slice_reduce_fusion
  60.4 0.1 eq.18
  60.4 1.3 dynamic-slice
  62.4 0.1 iota_add_fusion
  62.5 34.8 %all-gather.7.cloned.1.call-done = bf16[1024,1024]{1,0:T(8,128)(2,1)} async-done(((bf16[32,1024]{1,0:T(8,128)(2,1)}), bf16[1024,1024]{1,0:T(8,128)(2,1)}) %all-gather.7.cloned.1.call-update) | async-done | bytes 2097168 | tf_op jit(solution)/shard_map/all_gather | solution.py:49
  97.3 2.9 %copy.12 = bf16[1024,1024]{0,1:T(8,128)(2,1)S(1)} copy(bf16[1024,1024]{1,0:T(8,128)(2,1)} %all-gather.7.cloned.1.call-done) | data formatting | bytes 4194304 | tf_op jit(solution)/shard_map/all_gather | solution.py:49
  100.1 56.9 %all-gather.9.cloned.1.call-done = bf16[4096,251]{1,0:T(8,128)(2,1)} async-done(((bf16[256,251]{1,0:T(8,128)(2,1)}), bf16[4096,251]{1,0:T(8,128)(2,1)}) %all-gather.9.cloned.1.call-update) | async-done | bytes 2056208 | tf_op jit(solution)/shard_map/all_gather | solution.py:53
  157.0 5.9 %bitcast_reduce_fusion = (f32[1024]{0:T(1024)S(1)}, f32[1024,4,251,1]{0,2,1,3:T(8,128)}) fusion(bf16[1024,4,256,1]{0,2,3,1:T(8,128)(2,1)S(1)} %bitcast.46, bf16[4,4,256,251]{3,2,1,0:T(8,128)(2,1)} %bitcast.56), kind=kOutput, calls=%fused_computation.4 | convolution fusion | flops 2106567680 | bytes 8269824 | tf_op jit(solution)/shard_map/txd,xyde->tye/dot_general | solution.py:55
  162.9 0.1 stack.15
  163.0 2.9 %fusion.1 = (f32[1024]{0:T(1024)S(1)}, f32[1024]{0:T(1024)S(1)}, f32[1024]{0:T(1024)S(1)}) fusion(f32[1024,4,251,1]{0,2,1,3:T(8,128)} %get-tuple-element.16, f32[1024]{0:T(1024)S(1)} %get-tuple-element.15, s32[1024]{0:T(1024)S(1)} %eq.18, s32[4,251]{1,0:T(4,128)S(1)} %iota_add_fusion), kind=kLoop, calls=%fused_computation.6 | loop fusion | flops 7193600 | bytes 4136880 | tf_op jit(solution)/shard_map/reduce_sum | solution.py:65
  166.0 0.1 stack.18
  166.0 0.1 stack.17
  166.1 0.1 stack.16
  166.2 0.1 fusion.9
  166.3 0.7 reshape.155
  167.0 12.6 %all-to-all-start.1 = ((f32[32,1,128]{2,1,0:T(1,128)}), f32[32,1,128]{2,1,0:T(1,128)S(1)}, u32[]{:S(2)}, u32[]{:S(2)}) async-start(f32[32,1,128]{2,1,0:T(1,128)} %reshape.155), calls=%async_computation.1 | async-start | bytes 32768 | tf_op jit(solution)/shard_map/all_to_all | solution.py:70
  179.6 0.0 copy-done
  179.6 1.2 gather_fusion
  180.9 11.2 %all-to-all-done.1 = f32[32,1,128]{2,1,0:T(1,128)S(1)} async-done(((f32[32,1,128]{2,1,0:T(1,128)}), f32[32,1,128]{2,1,0:T(1,128)S(1)}, u32[]{:S(2)}, u32[]{:S(2)}) %all-to-all-start.1) | async-done | bytes 16416 | tf_op jit(solution)/shard_map/all_to_all | solution.py:70
  192.0 0.5 broadcast.223
  192.5 0.7 reduce.8
  193.2 0.1 reshape.156
  193.3 0.1 fusion.8
  193.5 0.1 subtract_dynamic-update-slice_fusion.1
  193.6 0.1 subtract_dynamic-update-slice_fusion
  193.7 8.6 %all-reduce.2 = (f32[128]{0:T(128)S(1)}, f32[128]{0:T(128)S(1)}) all-reduce(f32[128]{0:T(128)S(1)} %subtract_dynamic-update-slice_fusion.1, f32[128]{0:T(128)S(1)} %subtract_dynamic-update-slice_fusion), channel_id=1, replica_groups=mesh['x'=4,'y'=4,'z'=16,'c'=2] {'x'}, use_global_device_ids=true, to_apply=%add | all-reduce | flops 256 | bytes 2048
  202.2 0.5 broadcast_select_fusion
  202.8 0.5 broadcast_select_fusion.1
  (11 shorter events, 0.1 us)
Async XLA Ops:
  7.2 172.4 %copy-start = (s32[65]{0:T(128)S(1)}, s32[65]{0:T(128)}, u32[]{:S(2)}) copy-start(s32[65]{0:T(128)} %param.9) | copy-start | bytes 784
  7.2 15.2 %all-to-all-start = ((bf16[4,32,256]{2,1,0:T(8,128)(2,1)}), bf16[4,32,256]{2,1,0:T(8,128)(2,1)S(1)}, u32[]{:S(2)}, u32[]{:S(2)}) async-start(bf16[4,32,256]{2,1,0:T(8,128)(2,1)} %bitcast.53), calls=%async_computation | async-start | bytes 131072 | tf_op jit(solution)/shard_map/all_to_all | solution.py:41
  11.5 85.8 %all-gather.7.cloned.1.call-start = ((), (), s32[]{:S(2)}) async-start(), calls=%async_computation.2 | async-start | bytes 2162688 | tf_op jit(solution)/shard_map/all_gather | solution.py:49
  23.2 133.8 %all-gather.9.cloned.1.call-start = ((), (), s32[]{:S(2)}) async-start(), calls=%async_computation.3 | async-start | bytes 2228224 | tf_op jit(solution)/shard_map/all_gather | solution.py:53
  167.0 25.0 %all-to-all-start.1 = ((f32[32,1,128]{2,1,0:T(1,128)}), f32[32,1,128]{2,1,0:T(1,128)S(1)}, u32[]{:S(2)}, u32[]{:S(2)}) async-start(f32[32,1,128]{2,1,0:T(1,128)} %reshape.155), calls=%async_computation.1 | async-start | bytes 32768 | tf_op jit(solution)/shard_map/all_to_all | solution.py:70
Sparse Core Ops, SparseCore 0:
  23.4 73.8 all-gather.6
  100.3 56.7 all-gather.8
where the time goes:
time: 211 us; the launch traced here: 210 us
  waiting for transfers between devices  104 us (49%)
  blocking collectives  55 us (26%)
  starting transfers between devices  16.9 us (8%)
  between operations  14.8 us (7%)
  local copies, waits for them, and re-layouts  7.87 us (4%)
  other arithmetic  6.01 us (3%)
  matrix products  5.9 us (3%)
    all_gather x1, waiting for transfers between devices, per_device(): weight = lax.all_gather(head_weight, ('x', 'y'), axis=0)  56.9 us
    all_gather x1, blocking collectives, per_device(): group_ids = lax.all_gather(target_ids, TOKEN_AXES, axis=0)  36.2 us
    all_gather x1, waiting for transfers between devices, per_device(): group_rows = lax.all_gather(normed, TOKEN_AXES, axis=0, tiled=True)  34.8 us
    all_to_all x1, starting transfers between devices, per_device(): lax.all_to_all(stats, TOKEN_AXES, split_axis=1, concat_axis=1, tiled=True)  12.6 us
    all_to_all x1, waiting for transfers between devices, per_device(): lax.all_to_all(stats, TOKEN_AXES, split_axis=1, concat_axis=1, tiled=True)  11.2 us
    all_gather x1, blocking collectives, per_device(): gain_full = lax.all_gather(norm_gain, 'x', axis=0, tiled=True)  10.2 us
    unnamed x1, blocking collectives  8.57 us
    dot_general x1, matrix products, per_device(): jnp.einsum('txd,xyde->tye', group_rows.reshape(-1, x_count, D // x_count)...  5.9 us
  transfers between devices with their start and end apart: 4, of which 3 were waited for; matrix products, arithmetic and copies ran while one was open for 3% of the time, Pallas kernels for 0%

commit v1 on v0

--- a/solution.py
+++ b/solution.py
@@ -1,6 +1,8 @@
 import jax
 import jax.numpy as jnp
 from jax import lax
+from jax.experimental import pallas as pl
+from jax.experimental.pallas import tpu as pltpu
 from jax.sharding import Mesh
 from jax.sharding import PartitionSpec as P
 
@@ -20,6 +22,121 @@
     seq_index = jnp.where(is_long, 0, 1 + beyond // short_len)
     offset = jnp.where(is_long, positions, beyond % short_len)
     return offset < jnp.take(seq_lengths, seq_index)
+
+
+MESH_IDS = pl.DeviceIdType.MESH
+
+
+def gather_kernel(
+    normed_ref, weight_ref, ids_ref, normed_out, weight_out, ids_out,
+    row_send, row_recv, weight_send, weight_recv, id_send, id_recv, own_sems,
+):
+    x_count = lax.axis_size("x")
+    y_count = lax.axis_size("y")
+    z_count = lax.axis_size("z")
+    c_count = lax.axis_size("c")
+    x_index = lax.axis_index("x")
+    y_index = lax.axis_index("y")
+    z_index = lax.axis_index("z")
+    c_index = lax.axis_index("c")
+    row_group = z_count * c_count
+    weight_group = x_count * y_count
+    row_rank = z_index * c_count + c_index
+    weight_rank = x_index * y_count + y_index
+
+    def row_peer(step):
+        rank = lax.rem(row_rank + step, row_group)
+        return rank, (x_index, y_index, rank // c_count, rank % c_count)
+
+    def weight_peer(step):
+        rank = lax.rem(weight_rank + step, weight_group)
+        return rank, (rank // y_count, rank % y_count, z_index, c_index)
+
+    barrier = pltpu.get_barrier_semaphore()
+    for step in range(1, row_group):
+        pl.semaphore_signal(barrier, inc=1, device_id=row_peer(step)[1], device_id_type=MESH_IDS)
+    for step in range(1, weight_group):
+        pl.semaphore_signal(barrier, inc=1, device_id=weight_peer(step)[1], device_id_type=MESH_IDS)
+    pl.semaphore_wait(barrier, row_group - 1 + weight_group - 1)
+
+    own = [
+        pltpu.make_async_copy(normed_ref, normed_out.at[row_rank], own_sems.at[0]),
+        pltpu.make_async_copy(weight_ref, weight_out.at[weight_rank], own_sems.at[1]),
+        pltpu.make_async_copy(ids_ref, ids_out.at[row_rank], own_sems.at[2]),
+    ]
+    for copy in own:
+        copy.start()
+
+    sends = []
+    for step in range(1, weight_group):
+        _, device = weight_peer(step)
+        copy = pltpu.make_async_remote_copy(
+            src_ref=weight_ref, dst_ref=weight_out.at[weight_rank],
+            send_sem=weight_send.at[step - 1], recv_sem=weight_recv.at[weight_rank],
+            device_id=device, device_id_type=MESH_IDS,
+        )
+        copy.start()
+        sends.append(copy)
+    for step in range(1, row_group):
+        _, device = row_peer(step)
+        for src, dst, send_sem, recv_sem in (
+            (ids_ref, ids_out, id_send, id_recv),
+            (normed_ref, normed_out, row_send, row_recv),
+        ):
+            copy = pltpu.make_async_remote_copy(
+                src_ref=src, dst_ref=dst.at[row_rank],
+                send_sem=send_sem.at[step - 1], recv_sem=recv_sem.at[row_rank],
+                device_id=device, device_id_type=MESH_IDS,
+            )
+            copy.start()
+            sends.append(copy)
+
+    for copy in own:
+        copy.wait()
+    for copy in sends:
+        copy.wait_send()
+    for step in range(1, weight_group):
+        source = lax.rem(weight_rank + weight_group - step, weight_group)
+        pltpu.make_async_remote_copy(
+            src_ref=weight_ref, dst_ref=weight_out.at[source],
+            send_sem=weight_send.at[0], recv_sem=weight_recv.at[source],
+            device_id=weight_peer(step)[1], device_id_type=MESH_IDS,
+        ).wait_recv()
+    for step in range(1, row_group):
+        source = lax.rem(row_rank + row_group - step, row_group)
+        for src, dst, send_sem, recv_sem in (
+            (ids_ref, ids_out, id_send, id_recv),
+            (normed_ref, normed_out, row_send, row_recv),
+        ):
+            pltpu.make_async_remote_copy(
+                src_ref=src, dst_ref=dst.at[source],
+                send_sem=send_sem.at[0], recv_sem=recv_sem.at[source],
+                device_id=row_peer(step)[1], device_id_type=MESH_IDS,
+            ).wait_recv()
+
+
+def gather_groups(normed, weight, ids, row_group, weight_group):
+    any_spec = pl.BlockSpec(memory_space=pl.ANY)
+    return pl.pallas_call(
+        gather_kernel,
+        out_shape=(
+            jax.ShapeDtypeStruct((row_group,) + normed.shape, normed.dtype),
+            jax.ShapeDtypeStruct((weight_group,) + weight.shape, weight.dtype),
+            jax.ShapeDtypeStruct((row_group,) + ids.shape, ids.dtype),
+        ),
+        in_specs=[any_spec] * 3,
+        out_specs=(any_spec, any_spec, any_spec),
+        scratch_shapes=[
+            pltpu.SemaphoreType.DMA((row_group - 1,)),
+            pltpu.SemaphoreType.DMA((row_group,)),
+            pltpu.SemaphoreType.DMA((weight_group - 1,)),
+            pltpu.SemaphoreType.DMA((weight_group,)),
+            pltpu.SemaphoreType.DMA((row_group - 1,)),
+            pltpu.SemaphoreType.DMA((row_group,)),
+            pltpu.SemaphoreType.DMA((3,)),
+        ],
+        compiler_params=pltpu.CompilerParams(collective_id=0, has_side_effects=True),
+    )(normed, weight, ids)
 
 
 def per_device(hidden, norm_gain, head_weight, target_ids, seq_lengths):
@@ -46,11 +163,11 @@
         values * lax.rsqrt(squares / D + norm_epsilon) * gain_full.astype(jnp.float32)
     ).astype(jnp.bfloat16)
 
-    group_rows = lax.all_gather(normed, TOKEN_AXES, axis=0, tiled=True)
-    group_ids = lax.all_gather(target_ids, TOKEN_AXES, axis=0)
-    group_ids = lax.dynamic_slice_in_dim(group_ids, x_index * quarter, quarter, 1).reshape(-1)
-
-    weight = lax.all_gather(head_weight, ("x", "y"), axis=0)
+    group_rows, weight, group_ids = gather_groups(
+        normed, head_weight, target_ids.reshape(1, -1), group_count, x_count * y_count
+    )
+    group_rows = group_rows.reshape(-1, D)
+    group_ids = lax.dynamic_slice_in_dim(group_ids[:, 0, :], x_index * quarter, quarter, 1).reshape(-1)
     weight = weight.reshape(x_count, y_count, D // x_count, vocab_local)
     logits = jnp.einsum(
         "txd,xyde->tye",

time: 211 us -> 177 us (0.84)
  Pallas kernels: 0 us -> 109 us
  waiting for transfers between devices: 104 us -> 11.2 us
  blocking collectives: 55 us -> 17.9 us
  between operations: 14.8 us -> 1.43 us
    pallas_call x0 -> x1, Pallas kernels: none -> 109 us  [gather_groups(): pl.pallas_call(gather_kernel, out_shape=(jax.ShapeDtypeStruct((row_group,...]
    all_gather x2 -> x0, waiting for transfers between devices: 91.7 us -> none  [the longest x1 56.9 us: per_device(): weight = lax.all_gather(head_weight, ('x', 'y'), axis=0)]
    all_gather x1 -> x0, blocking collectives: 36.2 us -> none  [per_device(): group_ids = lax.all_gather(target_ids, TOKEN_AXES, axis=0)]
    another operation x0 -> x1, local copies, waits for them, and re-layouts: none -> 3.33 us  [per_device(): group_rows.reshape(-1, x_count, D // x_count)]
    all_gather x1 -> x0, local copies, waits for them, and re-layouts: 2.85 us -> none  [per_device(): group_rows = lax.all_gather(normed, TOKEN_AXES, axis=0, tiled=True)]
  transfers between devices with their start and end apart: 4 -> 2, of which waited for: 3 -> 1; matrix products, arithmetic and copies ran while one was open for 3% -> 2% of each run, Pallas kernels for 0% -> 0%
where the time goes in v1:
time: 177 us; the launch traced here: 176 us
  Pallas kernels  109 us (62%)
  blocking collectives  17.9 us (10%)
  starting transfers between devices  15.4 us (9%)
  waiting for transfers between devices  11.2 us (6%)
  local copies, waits for them, and re-layouts  9.07 us (5%)
  other arithmetic  6.01 us (3%)
  matrix products  5.91 us (3%)
    pallas_call x1, Pallas kernels, gather_groups(): pl.pallas_call(gather_kernel, out_shape=(jax.ShapeDtypeStruct((row_group,...  109 us
    all_to_all x1, waiting for transfers between devices, per_device(): lax.all_to_all(stats, TOKEN_AXES, split_axis=1, concat_axis=1, tiled=True)  11.2 us
    all_to_all x1, starting transfers between devices, per_device(): lax.all_to_all(stats, TOKEN_AXES, split_axis=1, concat_axis=1, tiled=True)  11.1 us
    all_gather x1, blocking collectives, per_device(): gain_full = lax.all_gather(norm_gain, 'x', axis=0, tiled=True)  10.2 us
    unnamed x1, blocking collectives  7.71 us
    dot_general x1, matrix products, per_device(): jnp.einsum('txd,xyde->tye', group_rows.reshape(-1, x_count, D // x_count)...  5.91 us
    all_to_all x1, starting transfers between devices, per_device(): rows = lax.all_to_all(hidden, 'x', split_axis=0, concat_axis=1, tiled=True)  4.3 us
  transfers between devices with their start and end apart: 2, of which 1 were waited for; matrix products, arithmetic and copies ran while one was open for 2% of the time, Pallas kernels for 0%

profile of v1, /device:TPU:24, one launch (start us, length us, event | category | flops | bytes accessed | tf_op | source)
XLA Modules:
  0.0 175.8 jit_solution(1038994287048713218)
XLA Ops:
  0.6 0.0 copy-start
  0.6 4.3 %all-to-all-start = ((bf16[4,32,256]{2,1,0:T(8,128)(2,1)}), bf16[4,32,256]{2,1,0:T(8,128)(2,1)S(1)}, u32[]{:S(2)}, u32[]{:S(2)}) async-start(bf16[4,32,256]{2,1,0:T(8,128)(2,1)} %bitcast.53), calls=%async_computation | async-start | bytes 131072 | tf_op jit(solution)/shard_map/all_to_all | solution.py:158
  5.0 0.1 iota_add_fusion
  5.1 0.7 reshape.133
  5.7 10.2 %all-gather = bf16[4,1,256]{2,1,0:T(2,128)(2,1)S(1)} all-gather(bf16[1,1,256]{2,1,0:T(2,128)(2,1)S(1)} %reshape.133), channel_id=1, replica_groups=mesh['x'=4,'y'=4,'z'=16,'c'=2] {'x'}, dimensions={0}, use_global_device_ids=true | all-gather | bytes 2560 | tf_op jit(solution)/shard_map/all_gather | solution.py:159
  15.9 1.3 dynamic-slice.1
  17.8 0.0 all-to-all-done
  17.9 0.1 fusion.7
  18.0 0.7 multiply_convert_fusion.normed_ref
  18.7 108.9 %shard_map.68 = (bf16[32,32,1024]{2,1,0:T(8,128)(2,1)}, bf16[16,256,251]{2,1,0:T(8,128)(2,1)}, s32[32,1,128]{2,1,0:T(1,128)}) custom-call(bf16[32,1024]{1,0:T(8,128)(2,1)} %multiply_convert_fusion.normed_ref, bf16[256,251]{1,0:T(8,128)(2,1)} %weight_ref.1, s32[1,128]{1,0:T(1,128)} %bitcast.55), custom_call_target="tpu_custom_call" | custom-call | tf_op jit(solution)/shard_map/pallas_call | solution.py:120
  127.6 0.8 dynamic-slice_reduce_fusion
  128.4 0.1 eq.18
  128.5 3.3 %reshape_reshape.3 = bf16[1024,4,256]{2,1,0:T(4,128)(2,1)S(1)} reshape(bf16[32,32,1024]{2,1,0:T(8,128)(2,1)} %get-tuple-element.5) | data formatting | bytes 4194304 | tf_op jit(solution)/shard_map/reshape;reshape | solution.py:174
  131.9 5.9 %bitcast_reduce_fusion = (f32[1024]{0:T(1024)S(1)}, f32[1024,4,251,1]{0,2,1,3:T(8,128)}) fusion(bf16[4,4,256,251]{3,2,1,0:T(8,128)(2,1)} %bitcast.56, bf16[1024,4,256]{2,1,0:T(4,128)(2,1)S(1)} %reshape_reshape.3), kind=kOutput, calls=%fused_computation.4 | convolution fusion | flops 2106567680 | bytes 8269824 | tf_op jit(solution)/shard_map/txd,xyde->tye/dot_general | solution.py:172
  137.8 0.1 stack.15
  137.9 2.9 %fusion.1 = (f32[1024]{0:T(1024)S(1)}, f32[1024]{0:T(1024)S(1)}, f32[1024]{0:T(1024)S(1)}) fusion(f32[1024,4,251,1]{0,2,1,3:T(8,128)} %get-tuple-element.22, f32[1024]{0:T(1024)S(1)} %get-tuple-element.21, s32[1024]{0:T(1024)S(1)} %eq.18, s32[4,251]{1,0:T(4,128)S(1)} %iota_add_fusion), kind=kLoop, calls=%fused_computation.6 | loop fusion | flops 7193600 | bytes 4136880 | tf_op jit(solution)/shard_map/reduce_sum | solution.py:182
  140.8 0.1 stack.16
  140.9 0.1 stack.17
  141.0 0.1 stack.18
  141.1 0.1 fusion.12
  141.1 0.7 reshape.149
  141.8 11.1 %all-to-all-start.1 = ((f32[32,1,128]{2,1,0:T(1,128)}), f32[32,1,128]{2,1,0:T(1,128)S(1)}, u32[]{:S(2)}, u32[]{:S(2)}) async-start(f32[32,1,128]{2,1,0:T(1,128)} %reshape.149), calls=%async_computation.1 | async-start | bytes 32768 | tf_op jit(solution)/shard_map/all_to_all | solution.py:187
  153.0 0.0 copy-done
  153.0 1.2 gather_fusion
  154.3 11.2 %all-to-all-done.1 = f32[32,1,128]{2,1,0:T(1,128)S(1)} async-done(((f32[32,1,128]{2,1,0:T(1,128)}), f32[32,1,128]{2,1,0:T(1,128)S(1)}, u32[]{:S(2)}, u32[]{:S(2)}) %all-to-all-start.1) | async-done | bytes 16416 | tf_op jit(solution)/shard_map/all_to_all | solution.py:187
  165.4 0.5 broadcast.223
  165.9 0.7 reduce.8
  166.6 0.1 reshape.150
  166.7 0.1 fusion.11
  166.9 0.1 subtract_dynamic-update-slice_fusion
  167.0 0.1 subtract_dynamic-update-slice_fusion.1
  167.1 7.7 %all-reduce.2 = (f32[128]{0:T(128)S(1)}, f32[128]{0:T(128)S(1)}) all-reduce(f32[128]{0:T(128)S(1)} %subtract_dynamic-update-slice_fusion.1, f32[128]{0:T(128)S(1)} %subtract_dynamic-update-slice_fusion), channel_id=1, replica_groups=mesh['x'=4,'y'=4,'z'=16,'c'=2] {'x'}, use_global_device_ids=true, to_apply=%add | all-reduce | flops 256 | bytes 2048
  174.8 0.5 broadcast_select_fusion
  175.3 0.5 broadcast_select_fusion.1
  (11 shorter events, 0.1 us)
Async XLA Ops:
  0.6 152.4 %copy-start = (s32[65]{0:T(128)S(1)}, s32[65]{0:T(128)}, u32[]{:S(2)}) copy-start(s32[65]{0:T(128)} %param.9) | copy-start | bytes 784
  0.6 17.2 %all-to-all-start = ((bf16[4,32,256]{2,1,0:T(8,128)(2,1)}), bf16[4,32,256]{2,1,0:T(8,128)(2,1)S(1)}, u32[]{:S(2)}, u32[]{:S(2)}) async-start(bf16[4,32,256]{2,1,0:T(8,128)(2,1)} %bitcast.53), calls=%async_computation | async-start | bytes 131072 | tf_op jit(solution)/shard_map/all_to_all | solution.py:158
  141.8 23.6 %all-to-all-start.1 = ((f32[32,1,128]{2,1,0:T(1,128)}), f32[32,1,128]{2,1,0:T(1,128)S(1)}, u32[]{:S(2)}, u32[]{:S(2)}) async-start(f32[32,1,128]{2,1,0:T(1,128)} %reshape.149), calls=%async_computation.1 | async-start | bytes 32768 | tf_op jit(solution)/shard_map/all_to_all | solution.py:187

commit v2 on v1

--- a/solution.py
+++ b/solution.py
@@ -43,18 +43,22 @@
     weight_group = x_count * y_count
     row_rank = z_index * c_count + c_index
     weight_rank = x_index * y_count + y_index
+    other_core = 1 - c_index
 
     def row_peer(step):
         rank = lax.rem(row_rank + step, row_group)
-        return rank, (x_index, y_index, rank // c_count, rank % c_count)
+        return (x_index, y_index, rank // c_count, rank % c_count)
 
     def weight_peer(step):
         rank = lax.rem(weight_rank + step, weight_group)
         return rank, (rank // y_count, rank % y_count, z_index, c_index)
 
+    def ring_z(shift):
+        return lax.rem(z_index + shift + z_count, z_count)
+
     barrier = pltpu.get_barrier_semaphore()
     for step in range(1, row_group):
-        pl.semaphore_signal(barrier, inc=1, device_id=row_peer(step)[1], device_id_type=MESH_IDS)
+        pl.semaphore_signal(barrier, inc=1, device_id=row_peer(step), device_id_type=MESH_IDS)
     for step in range(1, weight_group):
         pl.semaphore_signal(barrier, inc=1, device_id=weight_peer(step)[1], device_id_type=MESH_IDS)
     pl.semaphore_wait(barrier, row_group - 1 + weight_group - 1)
@@ -68,6 +72,42 @@
         copy.start()
 
     sends = []
+
+    def send_row(source_z, device, sem_index, from_input):
+        slot = source_z * c_count + c_index
+        copy = pltpu.make_async_remote_copy(
+            src_ref=normed_ref if from_input else normed_out.at[slot],
+            dst_ref=normed_out.at[slot],
+            send_sem=row_send.at[sem_index], recv_sem=row_recv.at[slot],
+            device_id=device, device_id_type=MESH_IDS,
+        )
+        copy.start()
+        sends.append(copy)
+
+    def wait_row(source_z, source_core):
+        slot = source_z * c_count + source_core
+        pltpu.make_async_remote_copy(
+            src_ref=normed_ref, dst_ref=normed_out.at[slot],
+            send_sem=row_send.at[0], recv_sem=row_recv.at[slot],
+            device_id=(x_index, y_index, z_index, other_core), device_id_type=MESH_IDS,
+        ).wait_recv()
+
+    right = (x_index, y_index, ring_z(1), c_index)
+    left = (x_index, y_index, ring_z(-1), c_index)
+    partner = (x_index, y_index, z_index, other_core)
+    right_steps = z_count // 2
+    left_steps = z_count - 1 - right_steps
+    sem_count = [0]
+
+    def next_sem():
+        sem_count[0] += 1
+        return sem_count[0] - 1
+
+    send_row(z_index, right, next_sem(), True)
+    if left_steps > 0:
+        send_row(z_index, left, next_sem(), True)
+    send_row(z_index, partner, next_sem(), True)
+
     for step in range(1, weight_group):
         _, device = weight_peer(step)
         copy = pltpu.make_async_remote_copy(
@@ -78,23 +118,31 @@
         copy.start()
         sends.append(copy)
     for step in range(1, row_group):
-        _, device = row_peer(step)
-        for src, dst, send_sem, recv_sem in (
-            (ids_ref, ids_out, id_send, id_recv),
-            (normed_ref, normed_out, row_send, row_recv),
-        ):
-            copy = pltpu.make_async_remote_copy(
-                src_ref=src, dst_ref=dst.at[row_rank],
-                send_sem=send_sem.at[step - 1], recv_sem=recv_sem.at[row_rank],
-                device_id=device, device_id_type=MESH_IDS,
-            )
-            copy.start()
-            sends.append(copy)
+        copy = pltpu.make_async_remote_copy(
+            src_ref=ids_ref, dst_ref=ids_out.at[row_rank],
+            send_sem=id_send.at[step - 1], recv_sem=id_recv.at[row_rank],
+            device_id=row_peer(step), device_id_type=MESH_IDS,
+        )
+        copy.start()
+        sends.append(copy)
+
+    for step in range(1, right_steps + 1):
+        from_left = ring_z(-step)
+        wait_row(from_left, c_index)
+        if step < right_steps:
+            send_row(from_left, right, next_sem(), False)
+        send_row(from_left, partner, next_sem(), False)
+        if step <= left_steps:
+            from_right = ring_z(step)
+            wait_row(from_right, c_index)
+            if step < left_steps:
+                send_row(from_right, left, next_sem(), False)
+            send_row(from_right, partner, next_sem(), False)
 
     for copy in own:
         copy.wait()
-    for copy in sends:
-        copy.wait_send()
+    for step in range(z_count):
+        wait_row(lax.rem(z_index + step, z_count), other_core)
     for step in range(1, weight_group):
         source = lax.rem(weight_rank + weight_group - step, weight_group)
         pltpu.make_async_remote_copy(
@@ -104,15 +152,13 @@
         ).wait_recv()
     for step in range(1, row_group):
         source = lax.rem(row_rank + row_group - step, row_group)
-        for src, dst, send_sem, recv_sem in (
-            (ids_ref, ids_out, id_send, id_recv),
-            (normed_ref, normed_out, row_send, row_recv),
-        ):
-            pltpu.make_async_remote_copy(
-                src_ref=src, dst_ref=dst.at[source],
-                send_sem=send_sem.at[0], recv_sem=recv_sem.at[source],
-                device_id=row_peer(step)[1], device_id_type=MESH_IDS,
-            ).wait_recv()
+        pltpu.make_async_remote_copy(
+            src_ref=ids_ref, dst_ref=ids_out.at[source],
+            send_sem=id_send.at[0], recv_sem=id_recv.at[source],
+            device_id=row_peer(step), device_id_type=MESH_IDS,
+        ).wait_recv()
+    for copy in sends:
+        copy.wait_send()
 
 
 def gather_groups(normed, weight, ids, row_group, weight_group):
@@ -155,9 +201,12 @@
     vocab_local = head_weight.shape[1]
     group_count = z_count * c_count
 
-    rows = lax.all_to_all(hidden, "x", split_axis=0, concat_axis=1, tiled=True)
-    gain_full = lax.all_gather(norm_gain, "x", axis=0, tiled=True)
-    values = rows.astype(jnp.float32)
+    pieces = hidden.reshape(x_count, quarter, -1)
+    gain_rows = jnp.broadcast_to(norm_gain[None, None, :], (x_count, 1, norm_gain.shape[0]))
+    pieces = jnp.concatenate([pieces, gain_rows], axis=1)
+    rows = lax.all_to_all(pieces, "x", split_axis=0, concat_axis=2, tiled=True)[0]
+    gain_full = rows[quarter]
+    values = rows[:quarter].astype(jnp.float32)
     squares = jnp.sum(values * values, axis=1, keepdims=True)
     normed = (
         values * lax.rsqrt(squares / D + norm_epsilon) * gain_full.astype(jnp.float32)

time: 177 us -> 119 us (0.67)
  Pallas kernels: 109 us -> 60 us
  blocking collectives: 17.9 us -> 9.23 us
  starting transfers between devices: 15.4 us -> 9.74 us
  waiting for transfers between devices: 11.2 us -> 14.9 us
    pallas_call x1, Pallas kernels: 109 us -> 60 us  [gather_groups(): pl.pallas_call(gather_kernel, out_shape=(jax.ShapeDtypeStruct((row_group,...]
    all_gather x1 -> x0, blocking collectives: 10.2 us -> none  [per_device(): gain_full = lax.all_gather(norm_gain, 'x', axis=0, tiled=True)]
    all_to_all x1, starting transfers between devices: 11.1 us -> 5.45 us  [per_device(): lax.all_to_all(stats, TOKEN_AXES, split_axis=1, concat_axis=1, tiled=True)]
    all_to_all x1, waiting for transfers between devices: 0.01 us -> 3.69 us  [per_device(): lax.all_to_all(pieces, 'x', split_axis=0, concat_axis=2, tiled=True)[0]]
  transfers between devices with their start and end apart: 2 -> 2, of which waited for: 1 -> 2; matrix products, arithmetic and copies ran while one was open for 2% -> 2% of each run, Pallas kernels for 0% -> 0%
where the time goes in v2:
time: 119 us; the launch traced here: 118 us
  Pallas kernels  60 us (50%)
  waiting for transfers between devices  14.9 us (13%)
  starting transfers between devices  9.74 us (8%)
  blocking collectives  9.23 us (8%)
  local copies, waits for them, and re-layouts  9.18 us (8%)
  other arithmetic  7.47 us (6%)
  matrix products  5.91 us (5%)
  between operations  1.44 us (1%)
    pallas_call x1, Pallas kernels, gather_groups(): pl.pallas_call(gather_kernel, out_shape=(jax.ShapeDtypeStruct((row_group,...  60 us
    all_to_all x1, waiting for transfers between devices, per_device(): lax.all_to_all(stats, TOKEN_AXES, split_axis=1, concat_axis=1, tiled=True)  11.2 us
    unnamed x1, blocking collectives  9.23 us
    dot_general x1, matrix products, per_device(): jnp.einsum('txd,xyde->tye', group_rows.reshape(-1, x_count, D // x_count)...  5.91 us
    all_to_all x1, starting transfers between devices, per_device(): lax.all_to_all(stats, TOKEN_AXES, split_axis=1, concat_axis=1, tiled=True)  5.45 us
    all_to_all x1, starting transfers between devices, per_device(): lax.all_to_all(pieces, 'x', split_axis=0, concat_axis=2, tiled=True)[0]  4.29 us
    all_to_all x1, waiting for transfers between devices, per_device(): lax.all_to_all(pieces, 'x', split_axis=0, concat_axis=2, tiled=True)[0]  3.69 us
    another operation x1, local copies, waits for them, and re-layouts, per_device(): group_rows.reshape(-1, x_count, D // x_count)  3.33 us
  transfers between devices with their start and end apart: 2, of which 2 were waited for; matrix products, arithmetic and copies ran while one was open for 2% of the time, Pallas kernels for 0%

profile of v2, /device:TPU:24, one launch (start us, length us, event | category | flops | bytes accessed | tf_op | source)
XLA Modules:
  0.0 117.8 jit_solution(17047463725877356971)
XLA Ops:
  0.6 0.0 copy-start
  0.6 0.7 broadcast_in_dim.28
  1.3 1.5 %pad_maximum_fusion = bf16[4,33,256]{2,1,0:T(8,128)(2,1)} fusion(bf16[4,1,256]{2,1,0:T(2,128)(2,1)S(1)} %broadcast_in_dim.28, bf16[4,32,256]{2,1,0:T(8,128)(2,1)} %bitcast.59), kind=kLoop, calls=%fused_computation.14 | loop fusion | flops 135168 | bytes 135168 | tf_op jit(solution)/shard_map/concatenate | solution.py:206
  2.8 4.3 %all-to-all-start = ((bf16[4,33,256]{2,1,0:T(8,128)(2,1)}), bf16[4,33,256]{2,1,0:T(8,128)(2,1)S(1)}, u32[]{:S(2)}, u32[]{:S(2)}) async-start(bf16[4,33,256]{2,1,0:T(8,128)(2,1)} %pad_maximum_fusion), calls=%async_computation | async-start | bytes 163840 | tf_op jit(solution)/shard_map/all_to_all | solution.py:207
  7.1 0.1 iota_add_fusion
  7.2 1.3 %dynamic-slice.1 = u32[1]{0:T(128)} dynamic-slice(u32[512]{0:T(512)} %constant.96, u32[]{:T(128)S(6)} %add.152), dynamic_slice_sizes={1} | dynamic-slice | bytes 12
  9.1 3.7 %all-to-all-done = bf16[4,33,256]{2,1,0:T(8,128)(2,1)S(1)} async-done(((bf16[4,33,256]{2,1,0:T(8,128)(2,1)}), bf16[4,33,256]{2,1,0:T(8,128)(2,1)S(1)}, u32[]{:S(2)}, u32[]{:S(2)}) %all-to-all-start) | async-done | bytes 67616 | tf_op jit(solution)/shard_map/all_to_all | solution.py:207
  12.8 0.1 multiply_reduce_fusion
  12.9 0.1 copy.13
  13.1 0.7 multiply_convert_fusion.normed_ref
  13.8 60.0 %shard_map.68 = (bf16[32,32,1024]{2,1,0:T(8,128)(2,1)}, bf16[16,256,251]{2,1,0:T(8,128)(2,1)}, s32[32,1,128]{2,1,0:T(1,128)}) custom-call(bf16[32,1024]{1,0:T(8,128)(2,1)} %multiply_convert_fusion.normed_ref, bf16[256,251]{1,0:T(8,128)(2,1)} %weight_ref.1, s32[1,128]{1,0:T(1,128)} %bitcast.61), custom_call_target="tpu_custom_call" | custom-call | tf_op jit(solution)/shard_map/pallas_call | solution.py:166
  73.7 0.8 dynamic-slice_reduce_fusion
  74.6 0.1 eq.18
  74.7 3.3 %reshape_reshape.3 = bf16[1024,4,256]{2,1,0:T(4,128)(2,1)S(1)} reshape(bf16[32,32,1024]{2,1,0:T(8,128)(2,1)} %get-tuple-element.5) | data formatting | bytes 4194304 | tf_op jit(solution)/shard_map/reshape;reshape | solution.py:223
  78.0 5.9 %bitcast_reduce_fusion = (f32[1024]{0:T(1024)S(1)}, f32[1024,4,251,1]{0,2,1,3:T(8,128)}) fusion(bf16[4,4,256,251]{3,2,1,0:T(8,128)(2,1)} %bitcast.62, bf16[1024,4,256]{2,1,0:T(4,128)(2,1)S(1)} %reshape_reshape.3), kind=kOutput, calls=%fused_computation.4 | convolution fusion | flops 2106567680 | bytes 8269824 | tf_op jit(solution)/shard_map/txd,xyde->tye/dot_general | solution.py:221
  83.9 0.1 stack.15
  84.0 2.9 %fusion.1 = (f32[1024]{0:T(1024)S(1)}, f32[1024]{0:T(1024)S(1)}, f32[1024]{0:T(1024)S(1)}) fusion(f32[1024,4,251,1]{0,2,1,3:T(8,128)} %get-tuple-element.22, f32[1024]{0:T(1024)S(1)} %get-tuple-element.21, s32[1024]{0:T(1024)S(1)} %eq.18, s32[4,251]{1,0:T(4,128)S(1)} %iota_add_fusion), kind=kLoop, calls=%fused_computation.6 | loop fusion | flops 7193600 | bytes 4136880 | tf_op jit(solution)/shard_map/reduce_sum | solution.py:231
  86.9 0.1 stack.16
  87.0 0.1 stack.17
  87.1 0.1 stack.18
  87.2 0.1 fusion.11
  87.3 0.7 reshape.161
  88.0 5.5 %all-to-all-start.1 = ((f32[32,1,128]{2,1,0:T(1,128)}), f32[32,1,128]{2,1,0:T(1,128)S(1)}, u32[]{:S(2)}, u32[]{:S(2)}) async-start(f32[32,1,128]{2,1,0:T(1,128)} %reshape.161), calls=%async_computation.1 | async-start | bytes 32768 | tf_op jit(solution)/shard_map/all_to_all | solution.py:236
  93.5 0.0 copy-done
  93.5 1.2 %gather_fusion = s32[128]{0:T(128)S(1)} fusion(s32[65]{0:T(128)S(1)} %copy-done, s32[1024]{0:T(1024)S(1)} %pad_clamp_fusion), kind=kCustom, calls=%fused_computation | custom fusion | bytes 1536 | tf_op jit(solution)/shard_map/jit(_take)/gather | solution.py:24
  94.7 11.2 %all-to-all-done.1 = f32[32,1,128]{2,1,0:T(1,128)S(1)} async-done(((f32[32,1,128]{2,1,0:T(1,128)}), f32[32,1,128]{2,1,0:T(1,128)S(1)}, u32[]{:S(2)}, u32[]{:S(2)}) %all-to-all-start.1) | async-done | bytes 16416 | tf_op jit(solution)/shard_map/all_to_all | solution.py:236
  105.9 0.5 broadcast.224
  106.4 0.7 reduce.7
  107.1 0.1 reshape.162
  107.2 0.1 fusion.10
  107.3 0.1 subtract_dynamic-update-slice_fusion
  107.4 0.1 subtract_dynamic-update-slice_fusion.1
  107.5 9.2 %all-reduce.2 = (f32[128]{0:T(128)S(1)}, f32[128]{0:T(128)S(1)}) all-reduce(f32[128]{0:T(128)S(1)} %subtract_dynamic-update-slice_fusion.1, f32[128]{0:T(128)S(1)} %subtract_dynamic-update-slice_fusion), channel_id=1, replica_groups=mesh['x'=4,'y'=4,'z'=16,'c'=2] {'x'}, use_global_device_ids=true, to_apply=%add | all-reduce | flops 256 | bytes 2048
  116.7 0.5 broadcast_select_fusion
  117.3 0.5 broadcast_select_fusion.1
  (11 shorter events, 0.1 us)
Async XLA Ops:
  0.6 92.8 %copy-start = (s32[65]{0:T(128)S(1)}, s32[65]{0:T(128)}, u32[]{:S(2)}) copy-start(s32[65]{0:T(128)} %param.9) | copy-start | bytes 784
  2.8 10.0 %all-to-all-start = ((bf16[4,33,256]{2,1,0:T(8,128)(2,1)}), bf16[4,33,256]{2,1,0:T(8,128)(2,1)S(1)}, u32[]{:S(2)}, u32[]{:S(2)}) async-start(bf16[4,33,256]{2,1,0:T(8,128)(2,1)} %pad_maximum_fusion), calls=%async_computation | async-start | bytes 163840 | tf_op jit(solution)/shard_map/all_to_all | solution.py:207
  88.0 17.9 %all-to-all-start.1 = ((f32[32,1,128]{2,1,0:T(1,128)}), f32[32,1,128]{2,1,0:T(1,128)S(1)}, u32[]{:S(2)}, u32[]{:S(2)}) async-start(f32[32,1,128]{2,1,0:T(1,128)} %reshape.161), calls=%async_computation.1 | async-start | bytes 32768 | tf_op jit(solution)/shard_map/all_to_all | solution.py:236

commit v3 on v2

--- a/solution.py
+++ b/solution.py
@@ -185,6 +185,83 @@
     )(normed, weight, ids)
 
 
+def stats_kernel(stats_ref, parts_out, send_sems, recv_sems, own_sem):
+    x_count = lax.axis_size("x")
+    z_count = lax.axis_size("z")
+    c_count = lax.axis_size("c")
+    x_index = lax.axis_index("x")
+    y_index = lax.axis_index("y")
+    z_index = lax.axis_index("z")
+    c_index = lax.axis_index("c")
+    group = z_count * c_count
+    total = x_count * group
+    rank = z_index * c_count + c_index
+    flat = x_index * group + rank
+
+    def peer(step):
+        other = lax.rem(flat + step, total)
+        member = other % group
+        return member, (other // group, y_index, member // c_count, member % c_count)
+
+    barrier = pltpu.get_barrier_semaphore()
+
+    def greet(step, carry):
+        pl.semaphore_signal(barrier, inc=1, device_id=peer(step)[1], device_id_type=MESH_IDS)
+        return carry
+
+    lax.fori_loop(1, total, greet, 0)
+    pl.semaphore_wait(barrier, total - 1)
+
+    own = pltpu.make_async_copy(stats_ref.at[rank], parts_out.at[x_index, rank], own_sem.at[0])
+    own.start()
+
+    def send_copy(step):
+        member, device = peer(step)
+        return pltpu.make_async_remote_copy(
+            src_ref=stats_ref.at[member], dst_ref=parts_out.at[x_index, rank],
+            send_sem=send_sems.at[step - 1], recv_sem=recv_sems.at[x_index, rank],
+            device_id=device, device_id_type=MESH_IDS,
+        )
+
+    def start(step, carry):
+        send_copy(step).start()
+        return carry
+
+    lax.fori_loop(1, total, start, 0)
+    own.wait()
+
+    def finish(step, carry):
+        send_copy(step).wait_send()
+        source = lax.rem(flat + total - step, total)
+        source_x = source // group
+        source_rank = source % group
+        pltpu.make_async_remote_copy(
+            src_ref=stats_ref.at[source_rank], dst_ref=parts_out.at[source_x, source_rank],
+            send_sem=send_sems.at[step - 1], recv_sem=recv_sems.at[source_x, source_rank],
+            device_id=peer(step)[1], device_id_type=MESH_IDS,
+        ).wait_recv()
+        return carry
+
+    lax.fori_loop(1, total, finish, 0)
+
+
+def exchange_stats(stats, x_count):
+    group = stats.shape[0]
+    any_spec = pl.BlockSpec(memory_space=pl.ANY)
+    return pl.pallas_call(
+        stats_kernel,
+        out_shape=jax.ShapeDtypeStruct((x_count,) + stats.shape, stats.dtype),
+        in_specs=[any_spec],
+        out_specs=any_spec,
+        scratch_shapes=[
+            pltpu.SemaphoreType.DMA((x_count * group - 1,)),
+            pltpu.SemaphoreType.DMA((x_count, group)),
+            pltpu.SemaphoreType.DMA((1,)),
+        ],
+        compiler_params=pltpu.CompilerParams(collective_id=1, has_side_effects=True),
+    )(stats)
+
+
 def per_device(hidden, norm_gain, head_weight, target_ids, seq_lengths):
     x_count = lax.axis_size("x")
     y_count = lax.axis_size("y")
@@ -233,20 +310,16 @@
     row_picked = jnp.sum(jnp.where(column_ids == group_ids[:, None, None], logits, 0.0), axis=(1, 2))
     stats = jnp.stack([row_peak, row_sum, row_weighted, row_picked]).reshape(4, group_count, quarter)
 
-    parts = lax.all_to_all(stats, TOKEN_AXES, split_axis=1, concat_axis=1, tiled=True)
-    part_peak, part_sum, part_weighted, part_picked = parts[0], parts[1], parts[2], parts[3]
-    highest = jnp.max(part_peak, axis=0)
-    factor = jnp.exp(part_peak - highest[None, :])
-    totals = jnp.sum(part_sum * factor, axis=0)
-    weighted = jnp.sum(part_weighted * factor, axis=0)
-    picked = jnp.sum(part_picked, axis=0)
+    parts = exchange_stats(stats.transpose(1, 0, 2), x_count)
+    part_peak, part_sum, part_weighted, part_picked = (parts[:, :, k] for k in range(4))
+    highest = jnp.max(part_peak, axis=1)
+    factor = jnp.exp(part_peak - highest[:, None])
+    totals = jnp.sum(part_sum * factor, axis=1)
+    weighted = jnp.sum(part_weighted * factor, axis=1)
+    picked = jnp.sum(part_picked, axis=1)
     log_norm = highest + jnp.log(totals)
-    logprob = picked - log_norm
-    entropy = log_norm - weighted / totals
-    full_logprob, full_entropy = (
-        lax.all_gather(logprob, "x", axis=0, tiled=True),
-        lax.all_gather(entropy, "x", axis=0, tiled=True),
-    )
+    full_logprob = (picked - log_norm).reshape(-1)
+    full_entropy = (log_norm - weighted / totals).reshape(-1)
     positions = vert_index * tok_local + jnp.arange(tok_local, dtype=jnp.int32)
     live_rows = live_mask(positions, seq_lengths, vert_count * tok_local // 2, SHORT)
     return (jnp.where(live_rows, full_logprob, 0.0), jnp.where(live_rows, full_entropy, 0.0))

time: 119 us -> 124 us (1.042)
  Pallas kernels: 60 us -> 92.2 us
  waiting for transfers between devices: 14.9 us -> 4.36 us
  blocking collectives: 9.23 us -> 0 us
  starting transfers between devices: 9.74 us -> 4.29 us
  local copies, waits for them, and re-layouts: 9.18 us -> 6.76 us
  other arithmetic: 7.47 us -> 8.77 us
    pallas_call x0 -> x1, Pallas kernels: none -> 32.3 us  [exchange_stats(): pl.pallas_call(stats_kernel, out_shape=jax.ShapeDtypeStruct((x_count,) +...]
    all_to_all x1 -> x0, waiting for transfers between devices: 11.2 us -> none  [per_device(): lax.all_to_all(stats, TOKEN_AXES, split_axis=1, concat_axis=1, tiled=True)]
    unnamed x1 -> x0, blocking collectives: 9.23 us -> none
    all_to_all x1 -> x0, starting transfers between devices: 5.45 us -> none  [per_device(): lax.all_to_all(stats, TOKEN_AXES, split_axis=1, concat_axis=1, tiled=True)]
    unnamed x8 -> x3, local copies, waits for them, and re-layouts: 2.1 us -> 0.04 us
    reduce_sum x1 -> x2, other arithmetic: 0.03 us -> 1.64 us  [the longest x1 1.59 us: per_device(): picked = jnp.sum(part_picked, axis=1)]
  transfers between devices with their start and end apart: 2 -> 1, of which waited for: 2 -> 1; matrix products, arithmetic and copies ran while one was open for 2% -> 1% of each run, Pallas kernels for 0% -> 0%
where the time goes in v3:
time: 124 us; the launch traced here: 123 us
  Pallas kernels  92.2 us (74%)
  other arithmetic  8.77 us (7%)
  local copies, waits for them, and re-layouts  6.76 us (5%)
  matrix products  5.91 us (5%)
  waiting for transfers between devices  4.36 us (4%)
  starting transfers between devices  4.29 us (3%)
    pallas_call x1, Pallas kernels, gather_groups(): pl.pallas_call(gather_kernel, out_shape=(jax.ShapeDtypeStruct((row_group,...  60 us
    pallas_call x1, Pallas kernels, exchange_stats(): pl.pallas_call(stats_kernel, out_shape=jax.ShapeDtypeStruct((x_count,) +...  32.3 us
    dot_general x1, matrix products, per_device(): jnp.einsum('txd,xyde->tye', group_rows.reshape(-1, x_count, D // x_count)...  5.91 us
    all_to_all x1, waiting for transfers between devices, per_device(): lax.all_to_all(pieces, 'x', split_axis=0, concat_axis=2, tiled=True)[0]  4.36 us
    all_to_all x1, starting transfers between devices, per_device(): lax.all_to_all(pieces, 'x', split_axis=0, concat_axis=2, tiled=True)[0]  4.29 us
    another operation x1, local copies, waits for them, and re-layouts, per_device(): group_rows.reshape(-1, x_count, D // x_count)  3.33 us
    reduce_sum x1, other arithmetic, per_device(): row_sum = jnp.sum(scaled, axis=(1, 2))  2.94 us
  transfers between devices with their start and end apart: 1, of which 1 were waited for; matrix products, arithmetic and copies ran while one was open for 1% of the time, Pallas kernels for 0%

profile of v3, /device:TPU:24, one launch (start us, length us, event | category | flops | bytes accessed | tf_op | source)
XLA Modules:
  0.0 123.1 jit_solution(6363088232902419114)
XLA Ops:
  0.6 0.0 copy-start
  0.6 0.7 broadcast_in_dim.28
  1.3 1.5 %pad_maximum_fusion = bf16[4,33,256]{2,1,0:T(8,128)(2,1)} fusion(bf16[4,1,256]{2,1,0:T(2,128)(2,1)S(1)} %broadcast_in_dim.28, bf16[4,32,256]{2,1,0:T(8,128)(2,1)} %bitcast.56), kind=kLoop, calls=%fused_computation.14 | loop fusion | flops 135168 | bytes 135168 | tf_op jit(solution)/shard_map/concatenate | solution.py:283
  2.8 4.3 %all-to-all-start = ((bf16[4,33,256]{2,1,0:T(8,128)(2,1)}), bf16[4,33,256]{2,1,0:T(8,128)(2,1)S(1)}, u32[]{:S(2)}, u32[]{:S(2)}) async-start(bf16[4,33,256]{2,1,0:T(8,128)(2,1)} %pad_maximum_fusion), calls=%async_computation | async-start | bytes 163840 | tf_op jit(solution)/shard_map/all_to_all | solution.py:284
  7.1 0.1 iota_add_fusion
  7.2 0.0 copy-done
  7.2 1.2 gather_fusion
  8.4 4.4 %all-to-all-done = bf16[4,33,256]{2,1,0:T(8,128)(2,1)S(1)} async-done(((bf16[4,33,256]{2,1,0:T(8,128)(2,1)}), bf16[4,33,256]{2,1,0:T(8,128)(2,1)S(1)}, u32[]{:S(2)}, u32[]{:S(2)}) %all-to-all-start) | async-done | bytes 67616 | tf_op jit(solution)/shard_map/all_to_all | solution.py:284
  12.8 0.1 multiply_reduce_fusion
  12.9 0.1 copy.17
  13.1 0.7 multiply_convert_fusion.normed_ref
  13.8 60.0 %shard_map.68 = (bf16[32,32,1024]{2,1,0:T(8,128)(2,1)}, bf16[16,256,251]{2,1,0:T(8,128)(2,1)}, s32[32,1,128]{2,1,0:T(1,128)}) custom-call(bf16[32,1024]{1,0:T(8,128)(2,1)} %multiply_convert_fusion.normed_ref, bf16[256,251]{1,0:T(8,128)(2,1)} %weight_ref.1, s32[1,128]{1,0:T(1,128)} %bitcast.58), custom_call_target="tpu_custom_call" | custom-call | tf_op jit(solution)/shard_map/pallas_call | solution.py:166
  73.7 0.8 dynamic-slice_reduce_fusion
  74.6 0.1 eq.18
  74.7 3.3 %reshape_reshape.3 = bf16[1024,4,256]{2,1,0:T(4,128)(2,1)S(1)} reshape(bf16[32,32,1024]{2,1,0:T(8,128)(2,1)} %get-tuple-element.5) | data formatting | bytes 4194304 | tf_op jit(solution)/shard_map/reshape;reshape | solution.py:300
  78.0 5.9 %bitcast_reduce_fusion = (f32[1024]{0:T(1024)S(1)}, f32[1024,4,251,1]{0,2,1,3:T(8,128)}) fusion(bf16[4,4,256,251]{3,2,1,0:T(8,128)(2,1)} %bitcast.59, bf16[1024,4,256]{2,1,0:T(4,128)(2,1)S(1)} %reshape_reshape.3), kind=kOutput, calls=%fused_computation.4 | convolution fusion | flops 2106567680 | bytes 8269824 | tf_op jit(solution)/shard_map/txd,xyde->tye/dot_general | solution.py:298
  83.9 0.1 stack.15
  84.0 2.9 %fusion.1 = (f32[1024]{0:T(1024)S(1)}, f32[1024]{0:T(1024)S(1)}, f32[1024]{0:T(1024)S(1)}) fusion(f32[1024,4,251,1]{0,2,1,3:T(8,128)} %get-tuple-element.22, f32[1024]{0:T(1024)S(1)} %get-tuple-element.21, s32[1024]{0:T(1024)S(1)} %eq.18, s32[4,251]{1,0:T(4,128)S(1)} %iota_add_fusion), kind=kLoop, calls=%fused_computation.6 | loop fusion | flops 7193600 | bytes 4136880 | tf_op jit(solution)/shard_map/reduce_sum | solution.py:308
  86.9 0.1 stack.16
  87.0 0.1 stack.17
  87.1 0.1 stack.18
  87.2 0.7 maximum_bitcast_fusion.stats_ref
  87.9 32.3 %shard_map.69 = f32[4,32,4,32]{3,2,1,0:T(4,128)} custom-call(f32[32,4,32]{2,1,0:T(4,128)} %maximum_bitcast_fusion.stats_ref), custom_call_target="tpu_custom_call" | custom-call | tf_op jit(solution)/shard_map/pallas_call | solution.py:251
  120.2 1.6 %slice_reduce_fusion = (f32[4,32]{1,0:T(4,128)S(1)}, f32[4,32,1,32]{3,2,1,0:T(1,128)S(1)}, f32[4,32,1,32]{3,2,1,0:T(1,128)S(1)}, f32[4,32,1,32]{3,2,1,0:T(1,128)S(1)}) fusion(f32[4,32,4,32]{3,2,1,0:T(4,128)} %shard_map.69), kind=kLoop, calls=%fused_computation.20 | loop fusion | flops 3968 | bytes 115200 | tf_op jit(solution)/shard_map/reduce_sum | solution.py:319
  121.9 0.1 sub.54
  122.0 0.1 sub.52
  122.0 0.5 broadcast_select_fusion
  122.6 0.5 broadcast_select_fusion.1
  (10 shorter events, 0.2 us)
Async XLA Ops:
  0.6 6.6 %copy-start = (s32[65]{0:T(128)S(1)}, s32[65]{0:T(128)}, u32[]{:S(2)}) copy-start(s32[65]{0:T(128)} %param.9) | copy-start | bytes 784
  2.8 10.0 %all-to-all-start = ((bf16[4,33,256]{2,1,0:T(8,128)(2,1)}), bf16[4,33,256]{2,1,0:T(8,128)(2,1)S(1)}, u32[]{:S(2)}, u32[]{:S(2)}) async-start(bf16[4,33,256]{2,1,0:T(8,128)(2,1)} %pad_maximum_fusion), calls=%async_computation | async-start | bytes 163840 | tf_op jit(solution)/shard_map/all_to_all | solution.py:284

commit v4 on v3

--- a/solution.py
+++ b/solution.py
@@ -185,7 +185,7 @@
     )(normed, weight, ids)
 
 
-def stats_kernel(stats_ref, parts_out, send_sems, recv_sems, own_sem):
+def stats_kernel(stats_ref, parts_out, merged, first_send, first_recv, second_send, second_recv, own_sems):
     x_count = lax.axis_size("x")
     z_count = lax.axis_size("z")
     c_count = lax.axis_size("c")
@@ -194,55 +194,76 @@
     z_index = lax.axis_index("z")
     c_index = lax.axis_index("c")
     group = z_count * c_count
-    total = x_count * group
     rank = z_index * c_count + c_index
-    flat = x_index * group + rank
-
-    def peer(step):
-        other = lax.rem(flat + step, total)
-        member = other % group
-        return member, (other // group, y_index, member // c_count, member % c_count)
+
+    def row_peer(step):
+        member = lax.rem(rank + step, group)
+        return member, (x_index, y_index, member // c_count, member % c_count)
+
+    def x_peer(step):
+        return (lax.rem(x_index + step, x_count), y_index, z_index, c_index)
 
     barrier = pltpu.get_barrier_semaphore()
 
     def greet(step, carry):
-        pl.semaphore_signal(barrier, inc=1, device_id=peer(step)[1], device_id_type=MESH_IDS)
+        pl.semaphore_signal(barrier, inc=1, device_id=row_peer(step)[1], device_id_type=MESH_IDS)
         return carry
 
-    lax.fori_loop(1, total, greet, 0)
-    pl.semaphore_wait(barrier, total - 1)
-
-    own = pltpu.make_async_copy(stats_ref.at[rank], parts_out.at[x_index, rank], own_sem.at[0])
+    lax.fori_loop(1, group, greet, 0)
+    for step in range(1, x_count):
+        pl.semaphore_signal(barrier, inc=1, device_id=x_peer(step), device_id_type=MESH_IDS)
+    pl.semaphore_wait(barrier, group - 1 + x_count - 1)
+
+    own = pltpu.make_async_copy(stats_ref.at[rank], merged.at[rank], own_sems.at[0])
     own.start()
 
-    def send_copy(step):
-        member, device = peer(step)
+    def first_copy(step):
+        member, device = row_peer(step)
         return pltpu.make_async_remote_copy(
-            src_ref=stats_ref.at[member], dst_ref=parts_out.at[x_index, rank],
-            send_sem=send_sems.at[step - 1], recv_sem=recv_sems.at[x_index, rank],
+            src_ref=stats_ref.at[member], dst_ref=merged.at[rank],
+            send_sem=first_send.at[step - 1], recv_sem=first_recv.at[rank],
             device_id=device, device_id_type=MESH_IDS,
         )
 
     def start(step, carry):
-        send_copy(step).start()
+        first_copy(step).start()
         return carry
 
-    lax.fori_loop(1, total, start, 0)
+    lax.fori_loop(1, group, start, 0)
     own.wait()
 
     def finish(step, carry):
-        send_copy(step).wait_send()
-        source = lax.rem(flat + total - step, total)
-        source_x = source // group
-        source_rank = source % group
-        pltpu.make_async_remote_copy(
-            src_ref=stats_ref.at[source_rank], dst_ref=parts_out.at[source_x, source_rank],
-            send_sem=send_sems.at[step - 1], recv_sem=recv_sems.at[source_x, source_rank],
-            device_id=peer(step)[1], device_id_type=MESH_IDS,
+        first_copy(step).wait_send()
+        source = lax.rem(rank + group - step, group)
+        pltpu.make_async_remote_copy(
+            src_ref=stats_ref.at[source], dst_ref=merged.at[source],
+            send_sem=first_send.at[step - 1], recv_sem=first_recv.at[source],
+            device_id=row_peer(step)[1], device_id_type=MESH_IDS,
         ).wait_recv()
         return carry
 
-    lax.fori_loop(1, total, finish, 0)
+    lax.fori_loop(1, group, finish, 0)
+
+    mine = pltpu.make_async_copy(merged, parts_out.at[x_index], own_sems.at[1])
+    mine.start()
+    copies = []
+    for step in range(1, x_count):
+        copy = pltpu.make_async_remote_copy(
+            src_ref=merged, dst_ref=parts_out.at[x_index],
+            send_sem=second_send.at[step - 1], recv_sem=second_recv.at[x_index],
+            device_id=x_peer(step), device_id_type=MESH_IDS,
+        )
+        copy.start()
+        copies.append(copy)
+    mine.wait()
+    for step in range(1, x_count):
+        copies[step - 1].wait_send()
+        source = lax.rem(x_index + x_count - step, x_count)
+        pltpu.make_async_remote_copy(
+            src_ref=merged, dst_ref=parts_out.at[source],
+            send_sem=second_send.at[step - 1], recv_sem=second_recv.at[source],
+            device_id=x_peer(x_count - step), device_id_type=MESH_IDS,
+        ).wait_recv()
 
 
 def exchange_stats(stats, x_count):
@@ -254,9 +275,12 @@
         in_specs=[any_spec],
         out_specs=any_spec,
         scratch_shapes=[
-            pltpu.SemaphoreType.DMA((x_count * group - 1,)),
-            pltpu.SemaphoreType.DMA((x_count, group)),
-            pltpu.SemaphoreType.DMA((1,)),
+            pltpu.VMEM(stats.shape, stats.dtype),
+            pltpu.SemaphoreType.DMA((group - 1,)),
+            pltpu.SemaphoreType.DMA((group,)),
+            pltpu.SemaphoreType.DMA((x_count - 1,)),
+            pltpu.SemaphoreType.DMA((x_count,)),
+            pltpu.SemaphoreType.DMA((2,)),
         ],
         compiler_params=pltpu.CompilerParams(collective_id=1, has_side_effects=True),
     )(stats)

time: 124 us -> 116 us (0.935)
  Pallas kernels: 92.2 us -> 84.6 us
    pallas_call x1, Pallas kernels: 32.3 us -> 24.6 us  [exchange_stats(): pl.pallas_call(stats_kernel, out_shape=jax.ShapeDtypeStruct((x_count,) +...]
where the time goes in v4:
time: 116 us; the launch traced here: 115 us
  Pallas kernels  84.6 us (73%)
  other arithmetic  8.77 us (8%)
  local copies, waits for them, and re-layouts  6.76 us (6%)
  matrix products  5.91 us (5%)
  waiting for transfers between devices  4.36 us (4%)
  starting transfers between devices  4.29 us (4%)
    pallas_call x1, Pallas kernels, gather_groups(): pl.pallas_call(gather_kernel, out_shape=(jax.ShapeDtypeStruct((row_group,...  60 us
    pallas_call x1, Pallas kernels, exchange_stats(): pl.pallas_call(stats_kernel, out_shape=jax.ShapeDtypeStruct((x_count,) +...  24.6 us
    dot_general x1, matrix products, per_device(): jnp.einsum('txd,xyde->tye', group_rows.reshape(-1, x_count, D // x_count)...  5.91 us
    all_to_all x1, waiting for transfers between devices, per_device(): lax.all_to_all(pieces, 'x', split_axis=0, concat_axis=2, tiled=True)[0]  4.36 us
    all_to_all x1, starting transfers between devices, per_device(): lax.all_to_all(pieces, 'x', split_axis=0, concat_axis=2, tiled=True)[0]  4.29 us
    another operation x1, local copies, waits for them, and re-layouts, per_device(): group_rows.reshape(-1, x_count, D // x_count)  3.33 us
    reduce_sum x1, other arithmetic, per_device(): row_sum = jnp.sum(scaled, axis=(1, 2))  2.94 us
  transfers between devices with their start and end apart: 1, of which 1 were waited for; matrix products, arithmetic and copies ran while one was open for 1% of the time, Pallas kernels for 0%

profile of v4, /device:TPU:24, one launch (start us, length us, event | category | flops | bytes accessed | tf_op | source)
XLA Modules:
  0.0 115.4 jit_solution(17227747188453520224)
XLA Ops:
  0.6 0.0 copy-start
  0.6 0.7 broadcast_in_dim.28
  1.3 1.5 %pad_maximum_fusion = bf16[4,33,256]{2,1,0:T(8,128)(2,1)} fusion(bf16[4,1,256]{2,1,0:T(2,128)(2,1)S(1)} %broadcast_in_dim.28, bf16[4,32,256]{2,1,0:T(8,128)(2,1)} %bitcast.56), kind=kLoop, calls=%fused_computation.14 | loop fusion | flops 135168 | bytes 135168 | tf_op jit(solution)/shard_map/concatenate | solution.py:307
  2.8 4.3 %all-to-all-start = ((bf16[4,33,256]{2,1,0:T(8,128)(2,1)}), bf16[4,33,256]{2,1,0:T(8,128)(2,1)S(1)}, u32[]{:S(2)}, u32[]{:S(2)}) async-start(bf16[4,33,256]{2,1,0:T(8,128)(2,1)} %pad_maximum_fusion), calls=%async_computation | async-start | bytes 163840 | tf_op jit(solution)/shard_map/all_to_all | solution.py:308
  7.1 0.1 iota_add_fusion
  7.2 0.0 copy-done
  7.2 1.2 %gather_fusion = s32[128]{0:T(128)S(1)} fusion(s32[65]{0:T(128)S(1)} %copy-done, s32[1024]{0:T(1024)S(1)} %pad_clamp_fusion), kind=kCustom, calls=%fused_computation | custom fusion | bytes 1536 | tf_op jit(solution)/shard_map/jit(_take)/gather | solution.py:24
  8.4 4.4 %all-to-all-done = bf16[4,33,256]{2,1,0:T(8,128)(2,1)S(1)} async-done(((bf16[4,33,256]{2,1,0:T(8,128)(2,1)}), bf16[4,33,256]{2,1,0:T(8,128)(2,1)S(1)}, u32[]{:S(2)}, u32[]{:S(2)}) %all-to-all-start) | async-done | bytes 67616 | tf_op jit(solution)/shard_map/all_to_all | solution.py:308
  12.8 0.1 multiply_reduce_fusion
  12.9 0.1 copy.17
  13.1 0.7 multiply_convert_fusion.normed_ref
  13.8 60.0 %shard_map.68 = (bf16[32,32,1024]{2,1,0:T(8,128)(2,1)}, bf16[16,256,251]{2,1,0:T(8,128)(2,1)}, s32[32,1,128]{2,1,0:T(1,128)}) custom-call(bf16[32,1024]{1,0:T(8,128)(2,1)} %multiply_convert_fusion.normed_ref, bf16[256,251]{1,0:T(8,128)(2,1)} %weight_ref.1, s32[1,128]{1,0:T(1,128)} %bitcast.58), custom_call_target="tpu_custom_call" | custom-call | tf_op jit(solution)/shard_map/pallas_call | solution.py:166
  73.7 0.8 dynamic-slice_reduce_fusion
  74.6 0.1 eq.18
  74.7 3.3 %reshape_reshape.3 = bf16[1024,4,256]{2,1,0:T(4,128)(2,1)S(1)} reshape(bf16[32,32,1024]{2,1,0:T(8,128)(2,1)} %get-tuple-element.5) | data formatting | bytes 4194304 | tf_op jit(solution)/shard_map/reshape;reshape | solution.py:324
  78.0 5.9 %bitcast_reduce_fusion = (f32[1024]{0:T(1024)S(1)}, f32[1024,4,251,1]{0,2,1,3:T(8,128)}) fusion(bf16[4,4,256,251]{3,2,1,0:T(8,128)(2,1)} %bitcast.59, bf16[1024,4,256]{2,1,0:T(4,128)(2,1)S(1)} %reshape_reshape.3), kind=kOutput, calls=%fused_computation.4 | convolution fusion | flops 2106567680 | bytes 8269824 | tf_op jit(solution)/shard_map/txd,xyde->tye/dot_general | solution.py:322
  83.9 0.1 stack.15
  84.0 2.9 %fusion.1 = (f32[1024]{0:T(1024)S(1)}, f32[1024]{0:T(1024)S(1)}, f32[1024]{0:T(1024)S(1)}) fusion(f32[1024,4,251,1]{0,2,1,3:T(8,128)} %get-tuple-element.22, f32[1024]{0:T(1024)S(1)} %get-tuple-element.21, s32[1024]{0:T(1024)S(1)} %eq.18, s32[4,251]{1,0:T(4,128)S(1)} %iota_add_fusion), kind=kLoop, calls=%fused_computation.6 | loop fusion | flops 7193600 | bytes 4136880 | tf_op jit(solution)/shard_map/reduce_sum | solution.py:332
  86.9 0.1 stack.16
  87.0 0.1 stack.17
  87.1 0.1 stack.18
  87.2 0.7 maximum_bitcast_fusion.stats_ref
  87.9 24.6 %shard_map.69 = f32[4,32,4,32]{3,2,1,0:T(4,128)} custom-call(f32[32,4,32]{2,1,0:T(4,128)} %maximum_bitcast_fusion.stats_ref), custom_call_target="tpu_custom_call" | custom-call | tf_op jit(solution)/shard_map/pallas_call | solution.py:272
  112.6 1.6 %slice_reduce_fusion = (f32[4,32]{1,0:T(4,128)S(1)}, f32[4,32,1,32]{3,2,1,0:T(1,128)S(1)}, f32[4,32,1,32]{3,2,1,0:T(1,128)S(1)}, f32[4,32,1,32]{3,2,1,0:T(1,128)S(1)}) fusion(f32[4,32,4,32]{3,2,1,0:T(4,128)} %shard_map.69), kind=kLoop, calls=%fused_computation.20 | loop fusion | flops 3968 | bytes 115200 | tf_op jit(solution)/shard_map/reduce_sum | solution.py:343
  114.2 0.1 sub.54
  114.3 0.1 sub.52
  114.4 0.5 broadcast_select_fusion
  114.9 0.5 broadcast_select_fusion.1
  (10 shorter events, 0.2 us)
Async XLA Ops:
  0.6 6.6 %copy-start = (s32[65]{0:T(128)S(1)}, s32[65]{0:T(128)}, u32[]{:S(2)}) copy-start(s32[65]{0:T(128)} %param.9) | copy-start | bytes 784
  2.8 10.0 %all-to-all-start = ((bf16[4,33,256]{2,1,0:T(8,128)(2,1)}), bf16[4,33,256]{2,1,0:T(8,128)(2,1)S(1)}, u32[]{:S(2)}, u32[]{:S(2)}) async-start(bf16[4,33,256]{2,1,0:T(8,128)(2,1)} %pad_maximum_fusion), calls=%async_computation | async-start | bytes 163840 | tf_op jit(solution)/shard_map/all_to_all | solution.py:308

commit v5 on v4

--- a/solution.py
+++ b/solution.py
@@ -28,7 +28,8 @@
 
 
 def gather_kernel(
-    normed_ref, weight_ref, ids_ref, normed_out, weight_out, ids_out,
+    hidden_ref, gain_ref, weight_ref, ids_ref, normed_out, weight_out, ids_out,
+    piece_vmem, gain_vmem, normed_vmem, piece_send, piece_recv, gain_send, gain_recv,
     row_send, row_recv, weight_send, weight_recv, id_send, id_recv, own_sems,
 ):
     x_count = lax.axis_size("x")
@@ -63,8 +64,34 @@
         pl.semaphore_signal(barrier, inc=1, device_id=weight_peer(step)[1], device_id_type=MESH_IDS)
     pl.semaphore_wait(barrier, row_group - 1 + weight_group - 1)
 
+    quarter = piece_vmem.shape[1]
+    width = piece_vmem.shape[2]
+
+    def x_peer(step):
+        return (lax.rem(x_index + step, x_count), y_index, z_index, c_index)
+
+    own_piece = pltpu.make_async_copy(
+        hidden_ref.at[pl.ds(x_index * quarter, quarter)], piece_vmem.at[x_index], own_sems.at[3]
+    )
+    own_gain = pltpu.make_async_copy(gain_ref, gain_vmem.at[x_index], own_sems.at[4])
+    own_piece.start()
+    own_gain.start()
+    piece_copies = []
+    for step in range(1, x_count):
+        target = lax.rem(x_index + step, x_count)
+        for src, dst, send_sem, recv_sem in (
+            (hidden_ref.at[pl.ds(target * quarter, quarter)], piece_vmem, piece_send, piece_recv),
+            (gain_ref, gain_vmem, gain_send, gain_recv),
+        ):
+            copy = pltpu.make_async_remote_copy(
+                src_ref=src, dst_ref=dst.at[x_index],
+                send_sem=send_sem.at[step - 1], recv_sem=recv_sem.at[x_index],
+                device_id=x_peer(step), device_id_type=MESH_IDS,
+            )
+            copy.start()
+            piece_copies.append(copy)
+
     own = [
-        pltpu.make_async_copy(normed_ref, normed_out.at[row_rank], own_sems.at[0]),
         pltpu.make_async_copy(weight_ref, weight_out.at[weight_rank], own_sems.at[1]),
         pltpu.make_async_copy(ids_ref, ids_out.at[row_rank], own_sems.at[2]),
     ]
@@ -76,7 +103,7 @@
     def send_row(source_z, device, sem_index, from_input):
         slot = source_z * c_count + c_index
         copy = pltpu.make_async_remote_copy(
-            src_ref=normed_ref if from_input else normed_out.at[slot],
+            src_ref=normed_out.at[slot],
             dst_ref=normed_out.at[slot],
             send_sem=row_send.at[sem_index], recv_sem=row_recv.at[slot],
             device_id=device, device_id_type=MESH_IDS,
@@ -87,7 +114,7 @@
     def wait_row(source_z, source_core):
         slot = source_z * c_count + source_core
         pltpu.make_async_remote_copy(
-            src_ref=normed_ref, dst_ref=normed_out.at[slot],
+            src_ref=normed_out.at[slot], dst_ref=normed_out.at[slot],
             send_sem=row_send.at[0], recv_sem=row_recv.at[slot],
             device_id=(x_index, y_index, z_index, other_core), device_id_type=MESH_IDS,
         ).wait_recv()
@@ -102,11 +129,6 @@
     def next_sem():
         sem_count[0] += 1
         return sem_count[0] - 1
-
-    send_row(z_index, right, next_sem(), True)
-    if left_steps > 0:
-        send_row(z_index, left, next_sem(), True)
-    send_row(z_index, partner, next_sem(), True)
 
     for step in range(1, weight_group):
         _, device = weight_peer(step)
@@ -125,6 +147,37 @@
         )
         copy.start()
         sends.append(copy)
+
+    own_piece.wait()
+    own_gain.wait()
+    for step in range(1, x_count):
+        source = lax.rem(x_index + x_count - step, x_count)
+        for src, dst, send_sem, recv_sem in (
+            (hidden_ref.at[pl.ds(0, quarter)], piece_vmem, piece_send, piece_recv),
+            (gain_ref, gain_vmem, gain_send, gain_recv),
+        ):
+            pltpu.make_async_remote_copy(
+                src_ref=src, dst_ref=dst.at[source],
+                send_sem=send_sem.at[step - 1], recv_sem=recv_sem.at[source],
+                device_id=x_peer(x_count - step), device_id_type=MESH_IDS,
+            ).wait_recv()
+    squares = jnp.zeros((quarter, 1), jnp.float32)
+    for part in range(x_count):
+        values = piece_vmem[part].astype(jnp.float32)
+        squares = squares + jnp.sum(values * values, axis=1, keepdims=True)
+    scale = lax.rsqrt(squares / (x_count * width) + norm_epsilon)
+    for part in range(x_count):
+        values = piece_vmem[part].astype(jnp.float32)
+        gain = gain_vmem[part].astype(jnp.float32)
+        normed_vmem[:, part * width:(part + 1) * width] = (values * scale * gain).astype(normed_vmem.dtype)
+    own_row = pltpu.make_async_copy(normed_vmem, normed_out.at[row_rank], own_sems.at[0])
+    own_row.start()
+    own_row.wait()
+
+    send_row(z_index, right, next_sem(), True)
+    if left_steps > 0:
+        send_row(z_index, left, next_sem(), True)
+    send_row(z_index, partner, next_sem(), True)
 
     for step in range(1, right_steps + 1):
         from_left = ring_z(-step)
@@ -157,32 +210,41 @@
             send_sem=id_send.at[0], recv_sem=id_recv.at[source],
             device_id=row_peer(step), device_id_type=MESH_IDS,
         ).wait_recv()
-    for copy in sends:
+    for copy in sends + piece_copies:
         copy.wait_send()
 
 
-def gather_groups(normed, weight, ids, row_group, weight_group):
+def gather_groups(hidden, gain, weight, ids, x_count, row_group, weight_group):
+    quarter = hidden.shape[0] // x_count
+    width = hidden.shape[1]
     any_spec = pl.BlockSpec(memory_space=pl.ANY)
     return pl.pallas_call(
         gather_kernel,
         out_shape=(
-            jax.ShapeDtypeStruct((row_group,) + normed.shape, normed.dtype),
+            jax.ShapeDtypeStruct((row_group, quarter, x_count * width), hidden.dtype),
             jax.ShapeDtypeStruct((weight_group,) + weight.shape, weight.dtype),
             jax.ShapeDtypeStruct((row_group,) + ids.shape, ids.dtype),
         ),
-        in_specs=[any_spec] * 3,
+        in_specs=[any_spec] * 4,
         out_specs=(any_spec, any_spec, any_spec),
         scratch_shapes=[
+            pltpu.VMEM((x_count, quarter, width), hidden.dtype),
+            pltpu.VMEM((x_count,) + gain.shape, gain.dtype),
+            pltpu.VMEM((quarter, x_count * width), hidden.dtype),
+            pltpu.SemaphoreType.DMA((x_count - 1,)),
+            pltpu.SemaphoreType.DMA((x_count,)),
+            pltpu.SemaphoreType.DMA((x_count - 1,)),
+            pltpu.SemaphoreType.DMA((x_count,)),
             pltpu.SemaphoreType.DMA((row_group - 1,)),
             pltpu.SemaphoreType.DMA((row_group,)),
             pltpu.SemaphoreType.DMA((weight_group - 1,)),
             pltpu.SemaphoreType.DMA((weight_group,)),
             pltpu.SemaphoreType.DMA((row_group - 1,)),
             pltpu.SemaphoreType.DMA((row_group,)),
-            pltpu.SemaphoreType.DMA((3,)),
+            pltpu.SemaphoreType.DMA((5,)),
         ],
         compiler_params=pltpu.CompilerParams(collective_id=0, has_side_effects=True),
-    )(normed, weight, ids)
+    )(hidden, gain, weight, ids)
 
 
 def stats_kernel(stats_ref, parts_out, merged, first_send, first_recv, second_send, second_recv, own_sems):
@@ -302,19 +364,9 @@
     vocab_local = head_weight.shape[1]
     group_count = z_count * c_count
 
-    pieces = hidden.reshape(x_count, quarter, -1)
-    gain_rows = jnp.broadcast_to(norm_gain[None, None, :], (x_count, 1, norm_gain.shape[0]))
-    pieces = jnp.concatenate([pieces, gain_rows], axis=1)
-    rows = lax.all_to_all(pieces, "x", split_axis=0, concat_axis=2, tiled=True)[0]
-    gain_full = rows[quarter]
-    values = rows[:quarter].astype(jnp.float32)
-    squares = jnp.sum(values * values, axis=1, keepdims=True)
-    normed = (
-        values * lax.rsqrt(squares / D + norm_epsilon) * gain_full.astype(jnp.float32)
-    ).astype(jnp.bfloat16)
-
     group_rows, weight, group_ids = gather_groups(
-        normed, head_weight, target_ids.reshape(1, -1), group_count, x_count * y_count
+        hidden, norm_gain.reshape(1, -1), head_weight, target_ids.reshape(1, -1),
+        x_count, group_count, x_count * y_count,
     )
     group_rows = group_rows.reshape(-1, D)
     group_ids = lax.dynamic_slice_in_dim(group_ids[:, 0, :], x_index * quarter, quarter, 1).reshape(-1)

time: 116 us -> 102 us (0.88)
  the two profiles are of different devices: /device:TPU:24 before, /device:TPU:16 now
where the time goes in v5:
time: 102 us
  Pallas kernels  85 us (83%)
  local copies, waits for them, and re-layouts  7.19 us (7%)
  other arithmetic  4.86 us (5%)
  matrix products  4.04 us (4%)
    pallas_call x1, Pallas kernels, gather_groups(): pl.pallas_call(gather_kernel, out_shape=(jax.ShapeDtypeStruct((row_group,...  54.1 us
    pallas_call x1, Pallas kernels, exchange_stats(): pl.pallas_call(stats_kernel, out_shape=jax.ShapeDtypeStruct((x_count,) +...  30.9 us
    dot_general x1, matrix products, per_device(): jnp.einsum('txd,xyde->tye', group_rows.reshape(-1, x_count, D // x_count)...  4.04 us
    another operation x1, local copies, waits for them, and re-layouts, per_device(): group_rows.reshape(-1, x_count, D // x_count)  3.33 us

profile of v5, /device:TPU:16, one launch (start us, length us, event | category | flops | bytes accessed | tf_op | source)
XLA Modules:
  0.0 101.8 jit_solution(10445206851495397699)
XLA Ops:
  0.6 0.0 copy-start
  0.7 1.2 %reshape.118.gain_ref = bf16[1,256]{1,0:T(2,128)(2,1)} reshape(bf16[256]{0:T(256)(128)(2,1)} %param.6) | data formatting | bytes 1024 | tf_op jit(solution)/shard_map/reshape | solution.py:368
  1.9 54.1 %shard_map.68 = (bf16[32,32,1024]{2,1,0:T(8,128)(2,1)}, bf16[16,256,251]{2,1,0:T(8,128)(2,1)}, s32[32,1,128]{2,1,0:T(1,128)}) custom-call(bf16[128,256]{1,0:T(8,128)(2,1)} %hidden_ref.1, bf16[1,256]{1,0:T(2,128)(2,1)} %reshape.118.gain_ref, bf16[256,251]{1,0:T(8,128)(2,1)} %weight_ref.1, s32[1,128]{1,0:T(1,128)} %bitcast.43), custom_call_target="tpu_custom_call" | custom-call | tf_op jit(solution)/shard_map/pallas_call | solution.py:221
  55.9 0.8 dynamic-slice_reduce_fusion
  56.8 0.1 eq.18
  56.9 0.1 iota_add_fusion
  56.9 3.3 %reshape_reshape.3 = bf16[1024,4,256]{2,1,0:T(4,128)(2,1)S(1)} reshape(bf16[32,32,1024]{2,1,0:T(8,128)(2,1)} %get-tuple-element.5) | data formatting | bytes 4194304 | tf_op jit(solution)/shard_map/reshape;reshape | solution.py:376
  60.3 4.0 %bitcast_reduce_fusion = (f32[1024]{0:T(1024)S(1)}, f32[1024,4,251,1]{0,2,1,3:T(8,128)S(1)}) fusion(bf16[4,4,256,251]{3,2,1,0:T(8,128)(2,1)} %bitcast.44, bf16[1024,4,256]{2,1,0:T(4,128)(2,1)S(1)} %reshape_reshape.3), kind=kOutput, calls=%fused_computation.4 | convolution fusion | flops 2106567680 | bytes 8269824 | tf_op jit(solution)/shard_map/txd,xyde->tye/dot_general | solution.py:374
  64.3 1.3 %fusion.1 = (f32[1024]{0:T(1024)S(1)}, f32[1024]{0:T(1024)S(1)}, f32[1024]{0:T(1024)S(1)}) fusion(f32[1024,4,251,1]{0,2,1,3:T(8,128)S(1)} %get-tuple-element.22, f32[1024]{0:T(1024)S(1)} %get-tuple-element.21, s32[1024]{0:T(1024)S(1)} %eq.18, s32[4,251]{1,0:T(4,128)S(1)} %iota_add_fusion), kind=kLoop, calls=%fused_computation.6 | loop fusion | flops 7193600 | bytes 4136880 | tf_op jit(solution)/shard_map/reduce_sum | solution.py:384
  65.7 0.1 stack.16
  65.8 0.1 stack.17
  65.8 0.1 stack.18
  65.9 0.1 stack.15
  66.0 0.7 maximum_bitcast_fusion.stats_ref
  66.7 30.9 %shard_map.69 = f32[4,32,4,32]{3,2,1,0:T(4,128)} custom-call(f32[32,4,32]{2,1,0:T(4,128)} %maximum_bitcast_fusion.stats_ref), custom_call_target="tpu_custom_call" | custom-call | tf_op jit(solution)/shard_map/pallas_call | solution.py:334
  97.7 1.6 %slice_reduce_fusion = (f32[4,32]{1,0:T(4,128)S(1)}, f32[4,32,1,32]{3,2,1,0:T(1,128)S(1)}, f32[4,32,1,32]{3,2,1,0:T(1,128)S(1)}, f32[4,32,1,32]{3,2,1,0:T(1,128)S(1)}) fusion(f32[4,32,4,32]{3,2,1,0:T(4,128)} %shard_map.69), kind=kLoop, calls=%fused_computation.16 | loop fusion | flops 3968 | bytes 115200 | tf_op jit(solution)/shard_map/reduce_sum | solution.py:395
  99.4 0.1 sub.54
  99.5 0.0 copy-done
  99.5 1.2 %gather_fusion = s32[128]{0:T(128)S(1)} fusion(s32[65]{0:T(128)S(1)} %copy-done, s32[1024]{0:T(1024)S(1)} %pad_clamp_fusion), kind=kCustom, calls=%fused_computation | custom fusion | bytes 1536 | tf_op jit(solution)/shard_map/jit(_take)/gather | solution.py:24
  100.7 0.5 broadcast_select_fusion
  101.2 0.1 sub.52
  101.3 0.5 broadcast_select_fusion.1
  (6 shorter events, 0.1 us)
Async XLA Ops:
  0.6 98.8 %copy-start = (s32[65]{0:T(128)S(1)}, s32[65]{0:T(128)}, u32[]{:S(2)}) copy-start(s32[65]{0:T(128)} %param.9) | copy-start | bytes 784

commit v6 on v5

--- a/solution.py
+++ b/solution.py
@@ -1,3 +1,5 @@
+import functools
+
 import jax
 import jax.numpy as jnp
 from jax import lax
@@ -247,8 +249,13 @@
     )(hidden, gain, weight, ids)
 
 
-def stats_kernel(stats_ref, parts_out, merged, first_send, first_recv, second_send, second_recv, own_sems):
+def stats_kernel(
+    vocab_local, rows_hbm, weight_hbm, local_ids, results_out,
+    rows_vmem, weight_vmem, spread, merged, result, first_send, first_recv,
+    second_send, second_recv, own_sems,
+):
     x_count = lax.axis_size("x")
+    y_count = lax.axis_size("y")
     z_count = lax.axis_size("z")
     c_count = lax.axis_size("c")
     x_index = lax.axis_index("x")
@@ -257,6 +264,9 @@
     c_index = lax.axis_index("c")
     group = z_count * c_count
     rank = z_index * c_count + c_index
+    quarter = spread.shape[2] // 4
+    width = weight_vmem.shape[1]
+    padded = weight_vmem.shape[2]
 
     def row_peer(step):
         member = lax.rem(rank + step, group)
@@ -274,15 +284,64 @@
     lax.fori_loop(1, group, greet, 0)
     for step in range(1, x_count):
         pl.semaphore_signal(barrier, inc=1, device_id=x_peer(step), device_id_type=MESH_IDS)
+
+    load_rows = pltpu.make_async_copy(rows_hbm, rows_vmem, own_sems.at[0])
+    load_weight = pltpu.make_async_copy(weight_hbm, weight_vmem, own_sems.at[1])
+    load_rows.start()
+    load_weight.start()
+    spread[...] = jnp.zeros_like(spread)
+    result[...] = jnp.zeros_like(result)
+    load_rows.wait()
+    load_weight.wait()
+
+    chunk = 256
+    slots_per_chunk = chunk // quarter
+    column = lax.broadcasted_iota(jnp.int32, (chunk, padded), 1)
+    valid = column < vocab_local
+    lane = lax.broadcasted_iota(jnp.int32, (chunk, 128), 1)
+    for first in range(0, rows_vmem.shape[0], chunk):
+        blocks = []
+        for y_block in range(y_count):
+            total = jnp.zeros((chunk, padded), jnp.float32)
+            for x_block in range(x_count):
+                total = total + jnp.dot(
+                    rows_vmem[first:first + chunk, x_block * width:(x_block + 1) * width],
+                    weight_vmem[x_block * y_count + y_block],
+                    preferred_element_type=jnp.float32,
+                )
+            blocks.append(total)
+        target = local_ids[first:first + chunk, 0:1]
+        peak = None
+        for y_block, block in enumerate(blocks):
+            block_peak = jnp.max(jnp.where(valid, block, -jnp.inf), axis=1, keepdims=True)
+            peak = block_peak if peak is None else jnp.maximum(peak, block_peak)
+        row_sum = jnp.zeros((chunk, 1), jnp.float32)
+        row_weighted = jnp.zeros((chunk, 1), jnp.float32)
+        row_picked = jnp.zeros((chunk, 1), jnp.float32)
+        for y_block, block in enumerate(blocks):
+            scaled = jnp.where(valid, jnp.exp(block - peak), 0.0)
+            row_sum = row_sum + jnp.sum(scaled, axis=1, keepdims=True)
+            row_weighted = row_weighted + jnp.sum(scaled * block, axis=1, keepdims=True)
+            hit = column + y_block * padded == target
+            row_picked = row_picked + jnp.sum(jnp.where(hit, block, 0.0), axis=1, keepdims=True)
+        table = jnp.where(
+            lane == 0, peak,
+            jnp.where(lane == 1, row_sum, jnp.where(lane == 2, row_weighted, jnp.where(lane == 3, row_picked, 0.0))),
+        )
+        lanes = table.T
+        for part in range(slots_per_chunk):
+            slot = first // quarter + part
+            spread[slot, :, 0:quarter] = lanes[0:8, part * quarter:(part + 1) * quarter]
+
     pl.semaphore_wait(barrier, group - 1 + x_count - 1)
 
-    own = pltpu.make_async_copy(stats_ref.at[rank], merged.at[rank], own_sems.at[0])
+    own = pltpu.make_async_copy(spread.at[rank], merged.at[rank], own_sems.at[2])
     own.start()
 
     def first_copy(step):
         member, device = row_peer(step)
         return pltpu.make_async_remote_copy(
-            src_ref=stats_ref.at[member], dst_ref=merged.at[rank],
+            src_ref=spread.at[member], dst_ref=merged.at[rank],
             send_sem=first_send.at[step - 1], recv_sem=first_recv.at[rank],
             device_id=device, device_id_type=MESH_IDS,
         )
@@ -298,7 +357,7 @@
         first_copy(step).wait_send()
         source = lax.rem(rank + group - step, group)
         pltpu.make_async_remote_copy(
-            src_ref=stats_ref.at[source], dst_ref=merged.at[source],
+            src_ref=spread.at[source], dst_ref=merged.at[source],
             send_sem=first_send.at[step - 1], recv_sem=first_recv.at[source],
             device_id=row_peer(step)[1], device_id_type=MESH_IDS,
         ).wait_recv()
@@ -306,12 +365,27 @@
 
     lax.fori_loop(1, group, finish, 0)
 
-    mine = pltpu.make_async_copy(merged, parts_out.at[x_index], own_sems.at[1])
+    highest = merged[0, 0:1, :]
+    for source in range(1, group):
+        highest = jnp.maximum(highest, merged[source, 0:1, :])
+    totals = jnp.zeros_like(highest)
+    weighted = jnp.zeros_like(highest)
+    picked = jnp.zeros_like(highest)
+    for source in range(group):
+        factor = jnp.exp(merged[source, 0:1, :] - highest)
+        totals = totals + merged[source, 1:2, :] * factor
+        weighted = weighted + merged[source, 2:3, :] * factor
+        picked = picked + merged[source, 3:4, :]
+    log_norm = highest + jnp.log(totals)
+    result[0:1, :] = picked - log_norm
+    result[1:2, :] = log_norm - weighted / totals
+
+    mine = pltpu.make_async_copy(result, results_out.at[x_index], own_sems.at[3])
     mine.start()
     copies = []
     for step in range(1, x_count):
         copy = pltpu.make_async_remote_copy(
-            src_ref=merged, dst_ref=parts_out.at[x_index],
+            src_ref=result, dst_ref=results_out.at[x_index],
             send_sem=second_send.at[step - 1], recv_sem=second_recv.at[x_index],
             device_id=x_peer(step), device_id_type=MESH_IDS,
         )
@@ -322,30 +396,34 @@
         copies[step - 1].wait_send()
         source = lax.rem(x_index + x_count - step, x_count)
         pltpu.make_async_remote_copy(
-            src_ref=merged, dst_ref=parts_out.at[source],
+            src_ref=result, dst_ref=results_out.at[source],
             send_sem=second_send.at[step - 1], recv_sem=second_recv.at[source],
             device_id=x_peer(x_count - step), device_id_type=MESH_IDS,
         ).wait_recv()
 
 
-def exchange_stats(stats, x_count):
-    group = stats.shape[0]
+def score_groups(rows, weight, local_ids, x_count, group, vocab_local):
+    quarter = rows.shape[0] // group
     any_spec = pl.BlockSpec(memory_space=pl.ANY)
     return pl.pallas_call(
-        stats_kernel,
-        out_shape=jax.ShapeDtypeStruct((x_count,) + stats.shape, stats.dtype),
-        in_specs=[any_spec],
+        functools.partial(stats_kernel, vocab_local),
+        out_shape=jax.ShapeDtypeStruct((x_count, 8, 128), jnp.float32),
+        in_specs=[any_spec, any_spec, pl.BlockSpec(memory_space=pltpu.VMEM)],
         out_specs=any_spec,
         scratch_shapes=[
-            pltpu.VMEM(stats.shape, stats.dtype),
+            pltpu.VMEM(rows.shape, rows.dtype),
+            pltpu.VMEM(weight.shape, weight.dtype),
+            pltpu.VMEM((group, 8, 128), jnp.float32),
+            pltpu.VMEM((group, 8, 128), jnp.float32),
+            pltpu.VMEM((8, 128), jnp.float32),
             pltpu.SemaphoreType.DMA((group - 1,)),
             pltpu.SemaphoreType.DMA((group,)),
             pltpu.SemaphoreType.DMA((x_count - 1,)),
             pltpu.SemaphoreType.DMA((x_count,)),
-            pltpu.SemaphoreType.DMA((2,)),
+            pltpu.SemaphoreType.DMA((4,)),
         ],
         compiler_params=pltpu.CompilerParams(collective_id=1, has_side_effects=True),
-    )(stats)
+    )(rows, weight, local_ids)
 
 
 def per_device(hidden, norm_gain, head_weight, target_ids, seq_lengths):
@@ -364,38 +442,23 @@
     vocab_local = head_weight.shape[1]
     group_count = z_count * c_count
 
+    padded = 128 * pl.cdiv(vocab_local, 128)
+    weight_padded = jnp.pad(head_weight, ((0, 0), (0, padded - vocab_local)))
     group_rows, weight, group_ids = gather_groups(
-        hidden, norm_gain.reshape(1, -1), head_weight, target_ids.reshape(1, -1),
+        hidden, norm_gain.reshape(1, -1), weight_padded, target_ids.reshape(1, -1),
         x_count, group_count, x_count * y_count,
     )
     group_rows = group_rows.reshape(-1, D)
     group_ids = lax.dynamic_slice_in_dim(group_ids[:, 0, :], x_index * quarter, quarter, 1).reshape(-1)
-    weight = weight.reshape(x_count, y_count, D // x_count, vocab_local)
-    logits = jnp.einsum(
-        "txd,xyde->tye",
-        group_rows.reshape(-1, x_count, D // x_count),
-        weight,
-        preferred_element_type=jnp.float32,
-    )
-    block_of = (lax.broadcasted_iota(jnp.int32, (1, y_count, vocab_local), 1) * z_count + z_index) * c_count + c_index
-    column_ids = block_of * vocab_local + lax.broadcasted_iota(jnp.int32, (1, y_count, vocab_local), 2)
-    row_peak = jnp.max(logits, axis=(1, 2))
-    scaled = jnp.exp(logits - row_peak[:, None, None])
-    row_sum = jnp.sum(scaled, axis=(1, 2))
-    row_weighted = jnp.sum(scaled * logits, axis=(1, 2))
-    row_picked = jnp.sum(jnp.where(column_ids == group_ids[:, None, None], logits, 0.0), axis=(1, 2))
-    stats = jnp.stack([row_peak, row_sum, row_weighted, row_picked]).reshape(4, group_count, quarter)
-
-    parts = exchange_stats(stats.transpose(1, 0, 2), x_count)
-    part_peak, part_sum, part_weighted, part_picked = (parts[:, :, k] for k in range(4))
-    highest = jnp.max(part_peak, axis=1)
-    factor = jnp.exp(part_peak - highest[:, None])
-    totals = jnp.sum(part_sum * factor, axis=1)
-    weighted = jnp.sum(part_weighted * factor, axis=1)
-    picked = jnp.sum(part_picked, axis=1)
-    log_norm = highest + jnp.log(totals)
-    full_logprob = (picked - log_norm).reshape(-1)
-    full_entropy = (log_norm - weighted / totals).reshape(-1)
+    target_block = group_ids // vocab_local
+    in_group = (target_block // c_count) % z_count == z_index
+    in_group = in_group & (target_block % c_count == c_index)
+    local_column = (target_block // (z_count * c_count)) * padded + group_ids % vocab_local
+    local_column = jnp.where(in_group, local_column, -1)
+    local_ids = jnp.broadcast_to(local_column[:, None], (local_column.shape[0], 128))
+    results = score_groups(group_rows, weight, local_ids, x_count, group_count, vocab_local)
+    full_logprob = results[:, 0, :quarter].reshape(-1)
+    full_entropy = results[:, 1, :quarter].reshape(-1)
     positions = vert_index * tok_local + jnp.arange(tok_local, dtype=jnp.int32)
     live_rows = live_mask(positions, seq_lengths, vert_count * tok_local // 2, SHORT)
     return (jnp.where(live_rows, full_logprob, 0.0), jnp.where(live_rows, full_entropy, 0.0))

time: 102 us -> 97.6 us (0.957)
  matrix products: 4.04 us -> 0 us
  Pallas kernels: 85 us -> 87.2 us
  other arithmetic: 4.86 us -> 2.88 us
    dot_general x1 -> x0, matrix products: 4.04 us -> none  [per_device(): jnp.einsum('txd,xyde->tye', group_rows.reshape(-1, x_count, D // x_count)...]
    another operation x5 -> x2, local copies, waits for them, and re-layouts: 3.67 us -> 0.17 us  [the longest x1 0.08 us: per_device(): full_entropy = results[:, 1, :quarter].reshape(-1)]
    reduce_sum x3 -> x0, other arithmetic: 2.98 us -> none  [the longest x1 1.59 us: per_device(): picked = jnp.sum(part_picked, axis=1)]
    pallas_call x1, Pallas kernels: 30.9 us -> 33.2 us  [score_groups(): pl.pallas_call(functools.partial(stats_kernel, vocab_local), out_shape=ja...]
    pad x0 -> x1, local copies, waits for them, and re-layouts: none -> 1.57 us  [per_device(): weight_padded = jnp.pad(head_weight, ((0, 0), (0, padded - vocab_local)))]
where the time goes in v6:
time: 97.6 us; the launch traced here: 97 us
  Pallas kernels  87.2 us (89%)
  local copies, waits for them, and re-layouts  6.21 us (6%)
  other arithmetic  2.88 us (3%)
    pallas_call x1, Pallas kernels, gather_groups(): pl.pallas_call(gather_kernel, out_shape=(jax.ShapeDtypeStruct((row_group,...  54.1 us
    pallas_call x1, Pallas kernels, score_groups(): pl.pallas_call(functools.partial(stats_kernel, vocab_local), out_shape=ja...  33.2 us

profile of v6, /device:TPU:16, one launch (start us, length us, event | category | flops | bytes accessed | tf_op | source)
XLA Modules:
  0.0 97.0 jit_solution(9429454543351082289)
XLA Ops:
  0.6 0.0 copy-start
  0.7 1.2 %reshape.158.gain_ref = bf16[1,256]{1,0:T(2,128)(2,1)} reshape(bf16[256]{0:T(256)(128)(2,1)} %param.6) | data formatting | bytes 1024 | tf_op jit(solution)/shard_map/reshape | solution.py:448
  1.9 0.0 copy-done
  1.9 1.2 %gather_fusion = s32[128]{0:T(128)S(1)} fusion(s32[65]{0:T(128)S(1)} %copy-done, s32[1024]{0:T(1024)S(1)} %pad_clamp_fusion), kind=kCustom, calls=%fused_computation | custom fusion | bytes 1536 | tf_op jit(solution)/shard_map/jit(_take)/gather | solution.py:26
  3.1 1.6 %pad.4.weight_ref = bf16[256,256]{1,0:T(8,128)(2,1)} pad(bf16[256,251]{1,0:T(8,128)(2,1)} %param.7, bf16[]{:T(256)} %constant.130.clone.1), padding=0_0x0_5 | pad | bytes 259586 | tf_op jit(solution)/shard_map/jit(_pad)/pad | solution.py:446
  4.7 54.1 %shard_map.68 = (bf16[32,32,1024]{2,1,0:T(8,128)(2,1)}, bf16[16,256,256]{2,1,0:T(8,128)(2,1)}, s32[32,1,128]{2,1,0:T(1,128)}) custom-call(bf16[128,256]{1,0:T(8,128)(2,1)} %hidden_ref.1, bf16[1,256]{1,0:T(2,128)(2,1)} %reshape.158.gain_ref, bf16[256,256]{1,0:T(8,128)(2,1)} %pad.4.weight_ref, s32[1,128]{1,0:T(1,128)} %bitcast.5), custom_call_target="tpu_custom_call" | custom-call | tf_op jit(solution)/shard_map/pallas_call | solution.py:223
  58.8 0.9 compare_reduce_fusion
  59.6 0.1 ne.143
  59.7 0.9 divide_reduce_fusion
  60.7 0.1 div.48
  60.7 0.1 rem.95
  60.8 1.0 %broadcast_in_dim.22.local_ids = s32[1024,128]{1,0:T(8,128)} broadcast(s32[1024]{0:T(1024)S(1)} %fusion.6), dimensions={0} | broadcast | bytes 528384 | tf_op jit(solution)/shard_map/broadcast_in_dim | solution.py:458
  61.8 33.2 %shard_map.69 = f32[4,8,128]{2,1,0:T(8,128)} custom-call(bf16[1024,1024]{1,0:T(8,128)(2,1)} %bitcast.4, bf16[16,256,256]{2,1,0:T(8,128)(2,1)} %get-tuple-element.6.weight_hbm, s32[1024,128]{1,0:T(8,128)} %broadcast_in_dim.22.local_ids), custom_call_target="tpu_custom_call" | custom-call | tf_op jit(solution)/shard_map/pallas_call | solution.py:408
  95.0 0.8 slice_reduce_fusion
  95.8 0.1 reshape_squeeze.7
  95.9 0.5 broadcast_select_fusion
  96.4 0.1 reshape_squeeze.6
  96.5 0.5 broadcast_select_fusion.1
  (3 shorter events, 0.0 us)
Async XLA Ops:
  0.6 1.3 %copy-start = (s32[65]{0:T(128)S(1)}, s32[65]{0:T(128)}, u32[]{:S(2)}) copy-start(s32[65]{0:T(128)} %param.9) | copy-start | bytes 784

commit v7 on v6

--- a/solution.py
+++ b/solution.py
@@ -29,10 +29,13 @@
 MESH_IDS = pl.DeviceIdType.MESH
 
 
-def gather_kernel(
-    hidden_ref, gain_ref, weight_ref, ids_ref, normed_out, weight_out, ids_out,
-    piece_vmem, gain_vmem, normed_vmem, piece_send, piece_recv, gain_send, gain_recv,
+def fused_kernel(
+    vocab_local, hidden_ref, gain_ref, weight_ref, ids_ref, results_out,
+    normed_out, weight_out, ids_out, piece_vmem, gain_vmem, normed_vmem,
+    spread, merged, result, ids_turned,
+    piece_send, piece_recv, gain_send, gain_recv,
     row_send, row_recv, weight_send, weight_recv, id_send, id_recv, own_sems,
+    first_send, first_recv, second_send, second_recv, stat_sems,
 ):
     x_count = lax.axis_size("x")
     y_count = lax.axis_size("y")
@@ -215,102 +218,38 @@
     for copy in sends + piece_copies:
         copy.wait_send()
 
-
-def gather_groups(hidden, gain, weight, ids, x_count, row_group, weight_group):
-    quarter = hidden.shape[0] // x_count
-    width = hidden.shape[1]
-    any_spec = pl.BlockSpec(memory_space=pl.ANY)
-    return pl.pallas_call(
-        gather_kernel,
-        out_shape=(
-            jax.ShapeDtypeStruct((row_group, quarter, x_count * width), hidden.dtype),
-            jax.ShapeDtypeStruct((weight_group,) + weight.shape, weight.dtype),
-            jax.ShapeDtypeStruct((row_group,) + ids.shape, ids.dtype),
-        ),
-        in_specs=[any_spec] * 4,
-        out_specs=(any_spec, any_spec, any_spec),
-        scratch_shapes=[
-            pltpu.VMEM((x_count, quarter, width), hidden.dtype),
-            pltpu.VMEM((x_count,) + gain.shape, gain.dtype),
-            pltpu.VMEM((quarter, x_count * width), hidden.dtype),
-            pltpu.SemaphoreType.DMA((x_count - 1,)),
-            pltpu.SemaphoreType.DMA((x_count,)),
-            pltpu.SemaphoreType.DMA((x_count - 1,)),
-            pltpu.SemaphoreType.DMA((x_count,)),
-            pltpu.SemaphoreType.DMA((row_group - 1,)),
-            pltpu.SemaphoreType.DMA((row_group,)),
-            pltpu.SemaphoreType.DMA((weight_group - 1,)),
-            pltpu.SemaphoreType.DMA((weight_group,)),
-            pltpu.SemaphoreType.DMA((row_group - 1,)),
-            pltpu.SemaphoreType.DMA((row_group,)),
-            pltpu.SemaphoreType.DMA((5,)),
-        ],
-        compiler_params=pltpu.CompilerParams(collective_id=0, has_side_effects=True),
-    )(hidden, gain, weight, ids)
-
-
-def stats_kernel(
-    vocab_local, rows_hbm, weight_hbm, local_ids, results_out,
-    rows_vmem, weight_vmem, spread, merged, result, first_send, first_recv,
-    second_send, second_recv, own_sems,
-):
-    x_count = lax.axis_size("x")
-    y_count = lax.axis_size("y")
-    z_count = lax.axis_size("z")
-    c_count = lax.axis_size("c")
-    x_index = lax.axis_index("x")
-    y_index = lax.axis_index("y")
-    z_index = lax.axis_index("z")
-    c_index = lax.axis_index("c")
-    group = z_count * c_count
-    rank = z_index * c_count + c_index
-    quarter = spread.shape[2] // 4
-    width = weight_vmem.shape[1]
-    padded = weight_vmem.shape[2]
-
-    def row_peer(step):
-        member = lax.rem(rank + step, group)
-        return member, (x_index, y_index, member // c_count, member % c_count)
-
-    def x_peer(step):
-        return (lax.rem(x_index + step, x_count), y_index, z_index, c_index)
-
-    barrier = pltpu.get_barrier_semaphore()
-
-    def greet(step, carry):
-        pl.semaphore_signal(barrier, inc=1, device_id=row_peer(step)[1], device_id_type=MESH_IDS)
-        return carry
-
-    lax.fori_loop(1, group, greet, 0)
-    for step in range(1, x_count):
-        pl.semaphore_signal(barrier, inc=1, device_id=x_peer(step), device_id_type=MESH_IDS)
-
-    load_rows = pltpu.make_async_copy(rows_hbm, rows_vmem, own_sems.at[0])
-    load_weight = pltpu.make_async_copy(weight_hbm, weight_vmem, own_sems.at[1])
-    load_rows.start()
-    load_weight.start()
+    group = row_group
+    rank = row_rank
+    width = weight_out.shape[1]
+    padded = weight_out.shape[2]
     spread[...] = jnp.zeros_like(spread)
     result[...] = jnp.zeros_like(result)
-    load_rows.wait()
-    load_weight.wait()
 
     chunk = 256
     slots_per_chunk = chunk // quarter
     column = lax.broadcasted_iota(jnp.int32, (chunk, padded), 1)
     valid = column < vocab_local
     lane = lax.broadcasted_iota(jnp.int32, (chunk, 128), 1)
-    for first in range(0, rows_vmem.shape[0], chunk):
+    for first in range(0, normed_out.shape[0] * quarter, chunk):
         blocks = []
         for y_block in range(y_count):
             total = jnp.zeros((chunk, padded), jnp.float32)
             for x_block in range(x_count):
+                rows = normed_out[first // quarter:(first + chunk) // quarter, :, x_block * width:(x_block + 1) * width]
                 total = total + jnp.dot(
-                    rows_vmem[first:first + chunk, x_block * width:(x_block + 1) * width],
-                    weight_vmem[x_block * y_count + y_block],
+                    rows.reshape(chunk, width),
+                    weight_out[x_block * y_count + y_block],
                     preferred_element_type=jnp.float32,
                 )
             blocks.append(total)
-        target = local_ids[first:first + chunk, 0:1]
+        id_rows = jnp.concatenate(
+            [ids_out[slot] for slot in range(first // quarter, first // quarter + slots_per_chunk)], axis=0
+        )
+        ids_turned[...] = id_rows.astype(jnp.float32).T
+        mine = ids_turned[pl.ds(pl.multiple_of(x_index * quarter, quarter), quarter), :]
+        target = jnp.concatenate(
+            [mine[:, part:part + 1] for part in range(slots_per_chunk)], axis=0
+        ).astype(jnp.int32)
         peak = None
         for y_block, block in enumerate(blocks):
             block_peak = jnp.max(jnp.where(valid, block, -jnp.inf), axis=1, keepdims=True)
@@ -322,7 +261,8 @@
             scaled = jnp.where(valid, jnp.exp(block - peak), 0.0)
             row_sum = row_sum + jnp.sum(scaled, axis=1, keepdims=True)
             row_weighted = row_weighted + jnp.sum(scaled * block, axis=1, keepdims=True)
-            hit = column + y_block * padded == target
+            global_id = ((y_block * z_count + z_index) * c_count + c_index) * vocab_local + column
+            hit = valid & (global_id == target)
             row_picked = row_picked + jnp.sum(jnp.where(hit, block, 0.0), axis=1, keepdims=True)
         table = jnp.where(
             lane == 0, peak,
@@ -333,13 +273,12 @@
             slot = first // quarter + part
             spread[slot, :, 0:quarter] = lanes[0:8, part * quarter:(part + 1) * quarter]
 
-    pl.semaphore_wait(barrier, group - 1 + x_count - 1)
-
-    own = pltpu.make_async_copy(spread.at[rank], merged.at[rank], own_sems.at[2])
+    own = pltpu.make_async_copy(spread.at[rank], merged.at[rank], stat_sems.at[0])
     own.start()
 
     def first_copy(step):
-        member, device = row_peer(step)
+        member = lax.rem(rank + step, group)
+        device = row_peer(step)
         return pltpu.make_async_remote_copy(
             src_ref=spread.at[member], dst_ref=merged.at[rank],
             send_sem=first_send.at[step - 1], recv_sem=first_recv.at[rank],
@@ -359,7 +298,7 @@
         pltpu.make_async_remote_copy(
             src_ref=spread.at[source], dst_ref=merged.at[source],
             send_sem=first_send.at[step - 1], recv_sem=first_recv.at[source],
-            device_id=row_peer(step)[1], device_id_type=MESH_IDS,
+            device_id=row_peer(step), device_id_type=MESH_IDS,
         ).wait_recv()
         return carry
 
@@ -380,7 +319,7 @@
     result[0:1, :] = picked - log_norm
     result[1:2, :] = log_norm - weighted / totals
 
-    mine = pltpu.make_async_copy(result, results_out.at[x_index], own_sems.at[3])
+    mine = pltpu.make_async_copy(result, results_out.at[x_index], stat_sems.at[1])
     mine.start()
     copies = []
     for step in range(1, x_count):
@@ -402,28 +341,45 @@
         ).wait_recv()
 
 
-def score_groups(rows, weight, local_ids, x_count, group, vocab_local):
-    quarter = rows.shape[0] // group
+def score_all(hidden, gain, weight, ids, x_count, row_group, weight_group, vocab_local):
+    quarter = hidden.shape[0] // x_count
+    width = hidden.shape[1]
     any_spec = pl.BlockSpec(memory_space=pl.ANY)
     return pl.pallas_call(
-        functools.partial(stats_kernel, vocab_local),
+        functools.partial(fused_kernel, vocab_local),
         out_shape=jax.ShapeDtypeStruct((x_count, 8, 128), jnp.float32),
-        in_specs=[any_spec, any_spec, pl.BlockSpec(memory_space=pltpu.VMEM)],
+        in_specs=[any_spec] * 4,
         out_specs=any_spec,
         scratch_shapes=[
-            pltpu.VMEM(rows.shape, rows.dtype),
-            pltpu.VMEM(weight.shape, weight.dtype),
-            pltpu.VMEM((group, 8, 128), jnp.float32),
-            pltpu.VMEM((group, 8, 128), jnp.float32),
+            pltpu.VMEM((row_group, quarter, x_count * width), hidden.dtype),
+            pltpu.VMEM((weight_group,) + weight.shape, weight.dtype),
+            pltpu.VMEM((row_group,) + ids.shape, ids.dtype),
+            pltpu.VMEM((x_count, quarter, width), hidden.dtype),
+            pltpu.VMEM((x_count,) + gain.shape, gain.dtype),
+            pltpu.VMEM((quarter, x_count * width), hidden.dtype),
+            pltpu.VMEM((row_group, 8, 128), jnp.float32),
+            pltpu.VMEM((row_group, 8, 128), jnp.float32),
             pltpu.VMEM((8, 128), jnp.float32),
-            pltpu.SemaphoreType.DMA((group - 1,)),
-            pltpu.SemaphoreType.DMA((group,)),
+            pltpu.VMEM((ids.shape[1], 8), jnp.float32),
             pltpu.SemaphoreType.DMA((x_count - 1,)),
             pltpu.SemaphoreType.DMA((x_count,)),
-            pltpu.SemaphoreType.DMA((4,)),
+            pltpu.SemaphoreType.DMA((x_count - 1,)),
+            pltpu.SemaphoreType.DMA((x_count,)),
+            pltpu.SemaphoreType.DMA((row_group - 1,)),
+            pltpu.SemaphoreType.DMA((row_group,)),
+            pltpu.SemaphoreType.DMA((weight_group - 1,)),
+            pltpu.SemaphoreType.DMA((weight_group,)),
+            pltpu.SemaphoreType.DMA((row_group - 1,)),
+            pltpu.SemaphoreType.DMA((row_group,)),
+            pltpu.SemaphoreType.DMA((5,)),
+            pltpu.SemaphoreType.DMA((row_group - 1,)),
+            pltpu.SemaphoreType.DMA((row_group,)),
+            pltpu.SemaphoreType.DMA((x_count - 1,)),
+            pltpu.SemaphoreType.DMA((x_count,)),
+            pltpu.SemaphoreType.DMA((2,)),
         ],
-        compiler_params=pltpu.CompilerParams(collective_id=1, has_side_effects=True),
-    )(rows, weight, local_ids)
+        compiler_params=pltpu.CompilerParams(collective_id=0, has_side_effects=True),
+    )(hidden, gain, weight, ids)
 
 
 def per_device(hidden, norm_gain, head_weight, target_ids, seq_lengths):
@@ -444,19 +400,10 @@
 
     padded = 128 * pl.cdiv(vocab_local, 128)
     weight_padded = jnp.pad(head_weight, ((0, 0), (0, padded - vocab_local)))
-    group_rows, weight, group_ids = gather_groups(
+    results = score_all(
         hidden, norm_gain.reshape(1, -1), weight_padded, target_ids.reshape(1, -1),
-        x_count, group_count, x_count * y_count,
+        x_count, group_count, x_count * y_count, vocab_local,
     )
-    group_rows = group_rows.reshape(-1, D)
-    group_ids = lax.dynamic_slice_in_dim(group_ids[:, 0, :], x_index * quarter, quarter, 1).reshape(-1)
-    target_block = group_ids // vocab_local
-    in_group = (target_block // c_count) % z_count == z_index
-    in_group = in_group & (target_block % c_count == c_index)
-    local_column = (target_block // (z_count * c_count)) * padded + group_ids % vocab_local
-    local_column = jnp.where(in_group, local_column, -1)
-    local_ids = jnp.broadcast_to(local_column[:, None], (local_column.shape[0], 128))
-    results = score_groups(group_rows, weight, local_ids, x_count, group_count, vocab_local)
     full_logprob = results[:, 0, :quarter].reshape(-1)
     full_entropy = results[:, 1, :quarter].reshape(-1)
     positions = vert_index * tok_local + jnp.arange(tok_local, dtype=jnp.int32)

time: 97.6 us -> 84.4 us (0.86)
  Pallas kernels: 87.2 us -> 77.3 us
  other arithmetic: 2.88 us -> 1.07 us
  local copies, waits for them, and re-layouts: 6.21 us -> 5.02 us
    pallas_call x2 -> x1, Pallas kernels: 87.2 us -> 77.3 us  [score_all(): pl.pallas_call(functools.partial(fused_kernel, vocab_local), out_shape=ja...]
    broadcast_in_dim x1 -> x0, local copies, waits for them, and re-layouts: 1 us -> none  [per_device(): jnp.broadcast_to(local_column[:, None], (local_column.shape[0], 128))]
where the time goes in v7:
time: 84.4 us; the launch traced here: 84.1 us
  Pallas kernels  77.3 us (92%)
  local copies, waits for them, and re-layouts  5.02 us (6%)
  other arithmetic  1.07 us (1%)
    pallas_call x1, Pallas kernels, score_all(): pl.pallas_call(functools.partial(fused_kernel, vocab_local), out_shape=ja...  77.3 us

profile of v7, /device:TPU:16, one launch (start us, length us, event | category | flops | bytes accessed | tf_op | source)
XLA Modules:
  0.0 84.1 jit_solution(1793599587433139481)
XLA Ops:
  0.6 0.0 copy-start
  0.6 1.2 %reshape.70.gain_ref = bf16[1,256]{1,0:T(2,128)(2,1)} reshape(bf16[256]{0:T(256)(128)(2,1)} %param.6) | data formatting | bytes 1024 | tf_op jit(solution)/shard_map/reshape | solution.py:404
  1.9 1.6 %pad.4.weight_ref = bf16[256,256]{1,0:T(8,128)(2,1)} pad(bf16[256,251]{1,0:T(8,128)(2,1)} %param.7, bf16[]{:T(256)} %constant.75.clone.1), padding=0_0x0_5 | pad | bytes 259586 | tf_op jit(solution)/shard_map/jit(_pad)/pad | solution.py:402
  3.4 77.3 %shard_map.68 = f32[4,8,128]{2,1,0:T(8,128)} custom-call(bf16[128,256]{1,0:T(8,128)(2,1)} %hidden_ref.1, bf16[1,256]{1,0:T(2,128)(2,1)} %reshape.70.gain_ref, bf16[256,256]{1,0:T(8,128)(2,1)} %pad.4.weight_ref, s32[1,128]{1,0:T(1,128)} %bitcast.3), custom_call_target="tpu_custom_call" | custom-call | tf_op jit(solution)/shard_map/pallas_call | solution.py:348
  80.8 0.8 slice_reduce_fusion
  81.6 0.1 reshape_squeeze.7
  81.7 0.0 copy-done
  81.7 1.2 %gather_fusion = s32[128]{0:T(128)S(1)} fusion(s32[65]{0:T(128)S(1)} %copy-done, s32[1024]{0:T(1024)S(1)} %pad_clamp_fusion), kind=kCustom, calls=%fused_computation | custom fusion | bytes 1536 | tf_op jit(solution)/shard_map/jit(_take)/gather | solution.py:26
  83.0 0.5 broadcast_select_fusion
  83.5 0.1 reshape_squeeze.6
  83.6 0.5 broadcast_select_fusion.1
  (2 shorter events, 0.0 us)
Async XLA Ops:
  0.6 81.1 %copy-start = (s32[65]{0:T(128)S(1)}, s32[65]{0:T(128)}, u32[]{:S(2)}) copy-start(s32[65]{0:T(128)} %param.9) | copy-start | bytes 784

commit v8 on v7

--- a/solution.py
+++ b/solution.py
@@ -225,6 +225,26 @@
     spread[...] = jnp.zeros_like(spread)
     result[...] = jnp.zeros_like(result)
 
+    own_stats = pltpu.make_async_copy(spread.at[rank], merged.at[rank], stat_sems.at[0])
+
+    def stats_copy(slot):
+        return pltpu.make_async_remote_copy(
+            src_ref=spread.at[slot], dst_ref=merged.at[rank],
+            send_sem=first_send.at[slot], recv_sem=first_recv.at[rank],
+            device_id=(x_index, y_index, slot // c_count, slot % c_count), device_id_type=MESH_IDS,
+        )
+
+    def send_chunk(first_slot):
+        for slot in range(first_slot, first_slot + slots_per_chunk):
+
+            @pl.when(slot != rank)
+            def _():
+                stats_copy(slot).start()
+
+            @pl.when(slot == rank)
+            def _():
+                own_stats.start()
+
     chunk = 256
     slots_per_chunk = chunk // quarter
     column = lax.broadcasted_iota(jnp.int32, (chunk, padded), 1)
@@ -272,32 +292,25 @@
         for part in range(slots_per_chunk):
             slot = first // quarter + part
             spread[slot, :, 0:quarter] = lanes[0:8, part * quarter:(part + 1) * quarter]
-
-    own = pltpu.make_async_copy(spread.at[rank], merged.at[rank], stat_sems.at[0])
-    own.start()
-
-    def first_copy(step):
-        member = lax.rem(rank + step, group)
-        device = row_peer(step)
-        return pltpu.make_async_remote_copy(
-            src_ref=spread.at[member], dst_ref=merged.at[rank],
-            send_sem=first_send.at[step - 1], recv_sem=first_recv.at[rank],
-            device_id=device, device_id_type=MESH_IDS,
-        )
-
-    def start(step, carry):
-        first_copy(step).start()
-        return carry
-
-    lax.fori_loop(1, group, start, 0)
-    own.wait()
+        if first > 0:
+            send_chunk(first // quarter - slots_per_chunk)
+    send_chunk(group - slots_per_chunk)
+
+    for slot in range(group):
+
+        @pl.when(slot != rank)
+        def _():
+            stats_copy(slot).wait_send()
+
+        @pl.when(slot == rank)
+        def _():
+            own_stats.wait()
 
     def finish(step, carry):
-        first_copy(step).wait_send()
         source = lax.rem(rank + group - step, group)
         pltpu.make_async_remote_copy(
             src_ref=spread.at[source], dst_ref=merged.at[source],
-            send_sem=first_send.at[step - 1], recv_sem=first_recv.at[source],
+            send_sem=first_send.at[source], recv_sem=first_recv.at[source],
             device_id=row_peer(step), device_id_type=MESH_IDS,
         ).wait_recv()
         return carry
@@ -372,7 +385,7 @@
             pltpu.SemaphoreType.DMA((row_group - 1,)),
             pltpu.SemaphoreType.DMA((row_group,)),
             pltpu.SemaphoreType.DMA((5,)),
-            pltpu.SemaphoreType.DMA((row_group - 1,)),
+            pltpu.SemaphoreType.DMA((row_group,)),
             pltpu.SemaphoreType.DMA((row_group,)),
             pltpu.SemaphoreType.DMA((x_count - 1,)),
             pltpu.SemaphoreType.DMA((x_count,)),

time: 84.4 us -> 81.7 us (0.968)
  the two profiles are of different devices: /device:TPU:16 before, /device:TPU:8 now
where the time goes in v8:
time: 81.7 us; the launch traced here: 81.3 us
  Pallas kernels  74.6 us (91%)
  local copies, waits for them, and re-layouts  5.02 us (6%)
  other arithmetic  1.07 us (1%)
    pallas_call x1, Pallas kernels, score_all(): pl.pallas_call(functools.partial(fused_kernel, vocab_local), out_shape=ja...  74.6 us

profile of v8, /device:TPU:8, one launch (start us, length us, event | category | flops | bytes accessed | tf_op | source)
XLA Modules:
  0.0 81.3 jit_solution(2784964702290519762)
XLA Ops:
  0.6 0.0 copy-start
  0.6 1.2 %reshape.70.gain_ref = bf16[1,256]{1,0:T(2,128)(2,1)} reshape(bf16[256]{0:T(256)(128)(2,1)} %param.6) | data formatting | bytes 1024 | tf_op jit(solution)/shard_map/reshape | solution.py:417
  1.9 1.6 %pad.4.weight_ref = bf16[256,256]{1,0:T(8,128)(2,1)} pad(bf16[256,251]{1,0:T(8,128)(2,1)} %param.7, bf16[]{:T(256)} %constant.75.clone.1), padding=0_0x0_5 | pad | bytes 259586 | tf_op jit(solution)/shard_map/jit(_pad)/pad | solution.py:415
  3.4 74.6 %shard_map.68 = f32[4,8,128]{2,1,0:T(8,128)} custom-call(bf16[128,256]{1,0:T(8,128)(2,1)} %hidden_ref.1, bf16[1,256]{1,0:T(2,128)(2,1)} %reshape.70.gain_ref, bf16[256,256]{1,0:T(8,128)(2,1)} %pad.4.weight_ref, s32[1,128]{1,0:T(1,128)} %bitcast.3), custom_call_target="tpu_custom_call" | custom-call | tf_op jit(solution)/shard_map/pallas_call | solution.py:361
  78.0 0.8 %slice_reduce_fusion = (f32[4,32]{1,0:T(4,128)S(1)}, f32[4,32]{1,0:T(4,128)S(1)}) fusion(f32[4,8,128]{2,1,0:T(8,128)} %shard_map.68), kind=kLoop, calls=%fused_computation.6 | loop fusion | bytes 2048 | tf_op jit(solution)/shard_map/slice | solution.py:421
  78.9 0.1 reshape_squeeze.7
  79.0 0.0 copy-done
  79.0 1.2 %gather_fusion = s32[128]{0:T(128)S(1)} fusion(s32[65]{0:T(128)S(1)} %copy-done, s32[1024]{0:T(1024)S(1)} %pad_clamp_fusion), kind=kCustom, calls=%fused_computation | custom fusion | bytes 1536 | tf_op jit(solution)/shard_map/jit(_take)/gather | solution.py:26
  80.2 0.5 broadcast_select_fusion
  80.7 0.1 reshape_squeeze.6
  80.8 0.5 broadcast_select_fusion.1
  (2 shorter events, 0.0 us)
Async XLA Ops:
  0.6 78.3 %copy-start = (s32[65]{0:T(128)S(1)}, s32[65]{0:T(128)}, u32[]{:S(2)}) copy-start(s32[65]{0:T(128)} %param.9) | copy-start | bytes 784

commit v9 on v8

--- a/solution.py
+++ b/solution.py
@@ -411,10 +411,8 @@
     vocab_local = head_weight.shape[1]
     group_count = z_count * c_count
 
-    padded = 128 * pl.cdiv(vocab_local, 128)
-    weight_padded = jnp.pad(head_weight, ((0, 0), (0, padded - vocab_local)))
     results = score_all(
-        hidden, norm_gain.reshape(1, -1), weight_padded, target_ids.reshape(1, -1),
+        hidden, norm_gain.reshape(1, -1), head_weight, target_ids.reshape(1, -1),
         x_count, group_count, x_count * y_count, vocab_local,
     )
     full_logprob = results[:, 0, :quarter].reshape(-1)

time: 81.7 us -> 80.2 us (0.982)
  local copies, waits for them, and re-layouts: 5.02 us -> 3.45 us
    pad x1 -> x0, local copies, waits for them, and re-layouts: 1.56 us -> none  [per_device(): weight_padded = jnp.pad(head_weight, ((0, 0), (0, padded - vocab_local)))]
where the time goes in v9:
time: 80.2 us; the launch traced here: 79.9 us
  Pallas kernels  74.7 us (93%)
  local copies, waits for them, and re-layouts  3.45 us (4%)
  other arithmetic  1.07 us (1%)
    pallas_call x1, Pallas kernels, score_all(): pl.pallas_call(functools.partial(fused_kernel, vocab_local), out_shape=ja...  74.7 us

profile of v9, /device:TPU:8, one launch (start us, length us, event | category | flops | bytes accessed | tf_op | source)
XLA Modules:
  0.0 79.9 jit_solution(5320108075327908580)
XLA Ops:
  0.6 0.0 copy-start
  0.6 1.2 %reshape.70.gain_ref = bf16[1,256]{1,0:T(2,128)(2,1)} reshape(bf16[256]{0:T(256)(128)(2,1)} %param.6) | data formatting | bytes 1024 | tf_op jit(solution)/shard_map/reshape | solution.py:415
  1.9 74.7 %shard_map.68 = f32[4,8,128]{2,1,0:T(8,128)} custom-call(bf16[128,256]{1,0:T(8,128)(2,1)} %hidden_ref.1, bf16[1,256]{1,0:T(2,128)(2,1)} %reshape.70.gain_ref, bf16[256,251]{1,0:T(8,128)(2,1)} %weight_ref.1, s32[1,128]{1,0:T(1,128)} %bitcast.3), custom_call_target="tpu_custom_call" | custom-call | tf_op jit(solution)/shard_map/pallas_call | solution.py:361
  76.6 0.8 %slice_reduce_fusion = (f32[4,32]{1,0:T(4,128)S(1)}, f32[4,32]{1,0:T(4,128)S(1)}) fusion(f32[4,8,128]{2,1,0:T(8,128)} %shard_map.68), kind=kLoop, calls=%fused_computation.6 | loop fusion | bytes 2048 | tf_op jit(solution)/shard_map/slice | solution.py:419
  77.4 0.1 reshape_squeeze.7
  77.5 0.0 copy-done
  77.5 1.2 %gather_fusion = s32[128]{0:T(128)S(1)} fusion(s32[65]{0:T(128)S(1)} %copy-done, s32[1024]{0:T(1024)S(1)} %pad_clamp_fusion), kind=kCustom, calls=%fused_computation | custom fusion | bytes 1536 | tf_op jit(solution)/shard_map/jit(_take)/gather | solution.py:26
  78.7 0.5 broadcast_select_fusion
  79.3 0.1 reshape_squeeze.6
  79.4 0.5 broadcast_select_fusion.1
  (2 shorter events, 0.0 us)
Async XLA Ops:
  0.6 76.9 %copy-start = (s32[65]{0:T(128)S(1)}, s32[65]{0:T(128)}, u32[]{:S(2)}) copy-start(s32[65]{0:T(128)} %param.9) | copy-start | bytes 784

commit v10 on v9

--- a/solution.py
+++ b/solution.py
@@ -30,7 +30,7 @@
 
 
 def fused_kernel(
-    vocab_local, hidden_ref, gain_ref, weight_ref, ids_ref, results_out,
+    vocab_local, hidden_ref, gain_ref, weight_ref, ids_ref, lengths_ref, results_out,
     normed_out, weight_out, ids_out, piece_vmem, gain_vmem, normed_vmem,
     spread, merged, result, ids_turned,
     piece_send, piece_recv, gain_send, gain_recv,
@@ -329,8 +329,19 @@
         weighted = weighted + merged[source, 2:3, :] * factor
         picked = picked + merged[source, 3:4, :]
     log_norm = highest + jnp.log(totals)
-    result[0:1, :] = picked - log_norm
-    result[1:2, :] = log_norm - weighted / totals
+
+    block_tokens = x_count * quarter
+    vert_index = (y_index * z_count + z_index) * c_count + c_index
+    long_len = y_count * z_count * c_count * block_tokens // 2
+    block_start = vert_index * block_tokens
+    in_long = block_start < long_len
+    sequence = jnp.where(in_long, 0, 1 + (block_start - long_len) // SHORT)
+    live_length = lengths_ref[sequence]
+    positions = block_start + x_index * quarter + lax.broadcasted_iota(jnp.int32, (1, 128), 1)
+    offsets = jnp.where(in_long, positions, jnp.maximum(positions - long_len, 0) % SHORT)
+    live = offsets < live_length
+    result[0:1, :] = jnp.where(live, picked - log_norm, 0.0)
+    result[1:2, :] = jnp.where(live, log_norm - weighted / totals, 0.0)
 
     mine = pltpu.make_async_copy(result, results_out.at[x_index], stat_sems.at[1])
     mine.start()
@@ -354,14 +365,14 @@
         ).wait_recv()
 
 
-def score_all(hidden, gain, weight, ids, x_count, row_group, weight_group, vocab_local):
+def score_all(hidden, gain, weight, ids, lengths, x_count, row_group, weight_group, vocab_local):
     quarter = hidden.shape[0] // x_count
     width = hidden.shape[1]
     any_spec = pl.BlockSpec(memory_space=pl.ANY)
     return pl.pallas_call(
         functools.partial(fused_kernel, vocab_local),
         out_shape=jax.ShapeDtypeStruct((x_count, 8, 128), jnp.float32),
-        in_specs=[any_spec] * 4,
+        in_specs=[any_spec] * 4 + [pl.BlockSpec(memory_space=pltpu.SMEM)],
         out_specs=any_spec,
         scratch_shapes=[
             pltpu.VMEM((row_group, quarter, x_count * width), hidden.dtype),
@@ -392,7 +403,7 @@
             pltpu.SemaphoreType.DMA((2,)),
         ],
         compiler_params=pltpu.CompilerParams(collective_id=0, has_side_effects=True),
-    )(hidden, gain, weight, ids)
+    )(hidden, gain, weight, ids, lengths)
 
 
 def per_device(hidden, norm_gain, head_weight, target_ids, seq_lengths):
@@ -412,14 +423,12 @@
     group_count = z_count * c_count
 
     results = score_all(
-        hidden, norm_gain.reshape(1, -1), head_weight, target_ids.reshape(1, -1),
+        hidden, norm_gain.reshape(1, -1), head_weight, target_ids.reshape(1, -1), seq_lengths,
         x_count, group_count, x_count * y_count, vocab_local,
     )
     full_logprob = results[:, 0, :quarter].reshape(-1)
     full_entropy = results[:, 1, :quarter].reshape(-1)
-    positions = vert_index * tok_local + jnp.arange(tok_local, dtype=jnp.int32)
-    live_rows = live_mask(positions, seq_lengths, vert_count * tok_local // 2, SHORT)
-    return (jnp.where(live_rows, full_logprob, 0.0), jnp.where(live_rows, full_entropy, 0.0))
+    return (full_logprob, full_entropy)
 
 
 def solution(mesh):

time: 80.2 us -> 79.6 us (level)
  other arithmetic: 1.07 us -> 0 us
    gather x1 -> x0, local copies, waits for them, and re-layouts: 1.23 us -> none  [live_mask(): return offset < jnp.take(seq_lengths, seq_index)]
    select_n x3 -> x0, other arithmetic: 1.06 us -> none  [the longest x1 0.53 us: per_device(): jnp.where(live_rows, full_entropy, 0.0)]
where the time goes in v10:
time: 79.6 us; the launch traced here: 79.2 us
  Pallas kernels  75.4 us (95%)
  local copies, waits for them, and re-layouts  3.22 us (4%)
    pallas_call x1, Pallas kernels, score_all(): pl.pallas_call(functools.partial(fused_kernel, vocab_local), out_shape=ja...  75.4 us

profile of v10, /device:TPU:8, one launch (start us, length us, event | category | flops | bytes accessed | tf_op | source)
XLA Modules:
  0.0 79.2 jit_solution(17368185903359653909)
XLA Ops:
  0.6 0.0 copy-start
  0.6 0.6 copy-done
  1.3 0.6 reshape.10.gain_ref
  1.9 75.4 %shard_map.68 = f32[4,8,128]{2,1,0:T(8,128)} custom-call(bf16[128,256]{1,0:T(8,128)(2,1)} %hidden_ref.1, bf16[1,256]{1,0:T(2,128)(2,1)} %reshape.10.gain_ref, bf16[256,251]{1,0:T(8,128)(2,1)} %weight_ref.1, s32[1,128]{1,0:T(1,128)} %bitcast.1, s32[65]{0:T(128)} %lengths_ref.1), custom_call_target="tpu_custom_call" | custom-call | tf_op jit(solution)/shard_map/pallas_call | solution.py:372
  77.2 0.8 %slice_reduce_fusion = (f32[4,32]{1,0:T(4,128)S(1)}, f32[4,32]{1,0:T(4,128)S(1)}) fusion(f32[4,8,128]{2,1,0:T(8,128)} %shard_map.68), kind=kLoop, calls=%fused_computation | loop fusion | bytes 2048 | tf_op jit(solution)/shard_map/slice | solution.py:430
  78.0 0.6 reshape_squeeze.7
  78.6 0.6 reshape_squeeze.6
Async XLA Ops:
  0.6 0.7 copy-start

commit v11 on v10

--- a/solution.py
+++ b/solution.py
@@ -215,8 +215,6 @@
             send_sem=id_send.at[0], recv_sem=id_recv.at[source],
             device_id=row_peer(step), device_id_type=MESH_IDS,
         ).wait_recv()
-    for copy in sends + piece_copies:
-        copy.wait_send()
 
     group = row_group
     rank = row_rank
@@ -296,15 +294,7 @@
             send_chunk(first // quarter - slots_per_chunk)
     send_chunk(group - slots_per_chunk)
 
-    for slot in range(group):
-
-        @pl.when(slot != rank)
-        def _():
-            stats_copy(slot).wait_send()
-
-        @pl.when(slot == rank)
-        def _():
-            own_stats.wait()
+    own_stats.wait()
 
     def finish(step, carry):
         source = lax.rem(rank + group - step, group)
@@ -363,6 +353,13 @@
             send_sem=second_send.at[step - 1], recv_sem=second_recv.at[source],
             device_id=x_peer(x_count - step), device_id_type=MESH_IDS,
         ).wait_recv()
+    for copy in sends + piece_copies:
+        copy.wait_send()
+    for slot in range(group):
+
+        @pl.when(slot != rank)
+        def _():
+            stats_copy(slot).wait_send()
 
 
 def score_all(hidden, gain, weight, ids, lengths, x_count, row_group, weight_group, vocab_local):

time: 79.6 us -> 77 us (0.967)
  the two profiles are of different devices: /device:TPU:8 before, /device:TPU:16 now
where the time goes in v11:
time: 77 us; the launch traced here: 76.6 us
  Pallas kernels  72.8 us (95%)
  local copies, waits for them, and re-layouts  3.22 us (4%)
    pallas_call x1, Pallas kernels, score_all(): pl.pallas_call(functools.partial(fused_kernel, vocab_local), out_shape=ja...  72.8 us

profile of v11, /device:TPU:16, one launch (start us, length us, event | category | flops | bytes accessed | tf_op | source)
XLA Modules:
  0.0 76.6 jit_solution(5084340772995826464)
XLA Ops:
  0.6 0.0 copy-start
  0.6 0.6 copy-done
  1.3 0.6 reshape.10.gain_ref
  1.9 72.8 %shard_map.68 = f32[4,8,128]{2,1,0:T(8,128)} custom-call(bf16[128,256]{1,0:T(8,128)(2,1)} %hidden_ref.1, bf16[1,256]{1,0:T(2,128)(2,1)} %reshape.10.gain_ref, bf16[256,251]{1,0:T(8,128)(2,1)} %weight_ref.1, s32[1,128]{1,0:T(1,128)} %bitcast.1, s32[65]{0:T(128)} %lengths_ref.1), custom_call_target="tpu_custom_call" | custom-call | tf_op jit(solution)/shard_map/pallas_call | solution.py:369
  74.6 0.8 %slice_reduce_fusion = (f32[4,32]{1,0:T(4,128)S(1)}, f32[4,32]{1,0:T(4,128)S(1)}) fusion(f32[4,8,128]{2,1,0:T(8,128)} %shard_map.68), kind=kLoop, calls=%fused_computation | loop fusion | bytes 2048 | tf_op jit(solution)/shard_map/slice | solution.py:427
  75.5 0.6 reshape_squeeze.7
  76.1 0.6 reshape_squeeze.6
Async XLA Ops:
  0.6 0.7 copy-start

commit v12 on v11

--- a/solution.py
+++ b/solution.py
@@ -78,7 +78,7 @@
     own_piece = pltpu.make_async_copy(
         hidden_ref.at[pl.ds(x_index * quarter, quarter)], piece_vmem.at[x_index], own_sems.at[3]
     )
-    own_gain = pltpu.make_async_copy(gain_ref, gain_vmem.at[x_index], own_sems.at[4])
+    own_gain = pltpu.make_async_copy(gain_ref, gain_vmem.at[pl.ds(x_index * width, width)], own_sems.at[4])
     own_piece.start()
     own_gain.start()
     piece_copies = []
@@ -89,7 +89,7 @@
             (gain_ref, gain_vmem, gain_send, gain_recv),
         ):
             copy = pltpu.make_async_remote_copy(
-                src_ref=src, dst_ref=dst.at[x_index],
+                src_ref=src, dst_ref=dst.at[x_index] if dst is piece_vmem else dst.at[pl.ds(x_index * width, width)],
                 send_sem=send_sem.at[step - 1], recv_sem=recv_sem.at[x_index],
                 device_id=x_peer(step), device_id_type=MESH_IDS,
             )
@@ -162,7 +162,7 @@
             (gain_ref, gain_vmem, gain_send, gain_recv),
         ):
             pltpu.make_async_remote_copy(
-                src_ref=src, dst_ref=dst.at[source],
+                src_ref=src, dst_ref=dst.at[source] if dst is piece_vmem else dst.at[pl.ds(source * width, width)],
                 send_sem=send_sem.at[step - 1], recv_sem=recv_sem.at[source],
                 device_id=x_peer(x_count - step), device_id_type=MESH_IDS,
             ).wait_recv()
@@ -173,7 +173,7 @@
     scale = lax.rsqrt(squares / (x_count * width) + norm_epsilon)
     for part in range(x_count):
         values = piece_vmem[part].astype(jnp.float32)
-        gain = gain_vmem[part].astype(jnp.float32)
+        gain = gain_vmem[pl.ds(part * width, width)].astype(jnp.float32).reshape(1, width)
         normed_vmem[:, part * width:(part + 1) * width] = (values * scale * gain).astype(normed_vmem.dtype)
     own_row = pltpu.make_async_copy(normed_vmem, normed_out.at[row_rank], own_sems.at[0])
     own_row.start()
@@ -376,7 +376,7 @@
             pltpu.VMEM((weight_group,) + weight.shape, weight.dtype),
             pltpu.VMEM((row_group,) + ids.shape, ids.dtype),
             pltpu.VMEM((x_count, quarter, width), hidden.dtype),
-            pltpu.VMEM((x_count,) + gain.shape, gain.dtype),
+            pltpu.VMEM((x_count * gain.shape[0],), gain.dtype),
             pltpu.VMEM((quarter, x_count * width), hidden.dtype),
             pltpu.VMEM((row_group, 8, 128), jnp.float32),
             pltpu.VMEM((row_group, 8, 128), jnp.float32),
@@ -420,7 +420,7 @@
     group_count = z_count * c_count
 
     results = score_all(
-        hidden, norm_gain.reshape(1, -1), head_weight, target_ids.reshape(1, -1), seq_lengths,
+        hidden, norm_gain, head_weight, target_ids.reshape(1, -1), seq_lengths,
         x_count, group_count, x_count * y_count, vocab_local,
     )
     full_logprob = results[:, 0, :quarter].reshape(-1)

time: 77 us -> 75.8 us (0.984)
  local copies, waits for them, and re-layouts: 3.22 us -> 2 us
where the time goes in v12:
time: 75.8 us; the launch traced here: 75.5 us
  Pallas kernels  72.8 us (96%)
  local copies, waits for them, and re-layouts  2 us (3%)
    pallas_call x1, Pallas kernels, score_all(): pl.pallas_call(functools.partial(fused_kernel, vocab_local), out_shape=ja...  72.8 us

profile of v12, /device:TPU:16, one launch (start us, length us, event | category | flops | bytes accessed | tf_op | source)
XLA Modules:
  0.0 75.5 jit_solution(4169115169106150277)
XLA Ops:
  0.6 72.8 %shard_map.68 = f32[4,8,128]{2,1,0:T(8,128)} custom-call(bf16[128,256]{1,0:T(8,128)(2,1)} %hidden_ref.1, bf16[256]{0:T(256)(128)(2,1)} %gain_ref.1, bf16[256,251]{1,0:T(8,128)(2,1)} %weight_ref.1, s32[1,128]{1,0:T(1,128)} %bitcast.1, s32[65]{0:T(128)} %lengths_ref.1), custom_call_target="tpu_custom_call" | custom-call | tf_op jit(solution)/shard_map/pallas_call | solution.py:369
  73.5 0.8 %slice_reduce_fusion = (f32[4,32]{1,0:T(4,128)S(1)}, f32[4,32]{1,0:T(4,128)S(1)}) fusion(f32[4,8,128]{2,1,0:T(8,128)} %shard_map.68), kind=kLoop, calls=%fused_computation | loop fusion | bytes 2048 | tf_op jit(solution)/shard_map/slice | solution.py:427
  74.3 0.6 reshape_squeeze.7
  74.9 0.6 reshape_squeeze.6

commit v13 on v12

--- a/solution.py
+++ b/solution.py
@@ -243,7 +243,7 @@
             def _():
                 own_stats.start()
 
-    chunk = 256
+    chunk = 128
     slots_per_chunk = chunk // quarter
     column = lax.broadcasted_iota(jnp.int32, (chunk, padded), 1)
     valid = column < vocab_local
@@ -381,7 +381,7 @@
             pltpu.VMEM((row_group, 8, 128), jnp.float32),
             pltpu.VMEM((row_group, 8, 128), jnp.float32),
             pltpu.VMEM((8, 128), jnp.float32),
-            pltpu.VMEM((ids.shape[1], 8), jnp.float32),
+            pltpu.VMEM((ids.shape[1], 4), jnp.float32),
             pltpu.SemaphoreType.DMA((x_count - 1,)),
             pltpu.SemaphoreType.DMA((x_count,)),
             pltpu.SemaphoreType.DMA((x_count - 1,)),

time: 75.8 us -> 75.3 us (level)
  the two profiles are of different devices: /device:TPU:16 before, /device:TPU:400 now
where the time goes in v13:
time: 75.3 us; the launch traced here: 75 us
  Pallas kernels  72.4 us (96%)
  local copies, waits for them, and re-layouts  2 us (3%)
    pallas_call x1, Pallas kernels, score_all(): pl.pallas_call(functools.partial(fused_kernel, vocab_local), out_shape=ja...  72.4 us

profile of v13, /device:TPU:400, one launch (start us, length us, event | category | flops | bytes accessed | tf_op | source)
XLA Modules:
  0.0 75.0 jit_solution(10773143153111259537)
XLA Ops:
  0.6 72.4 %shard_map.68 = f32[4,8,128]{2,1,0:T(8,128)} custom-call(bf16[128,256]{1,0:T(8,128)(2,1)} %hidden_ref.1, bf16[256]{0:T(256)(128)(2,1)} %gain_ref.1, bf16[256,251]{1,0:T(8,128)(2,1)} %weight_ref.1, s32[1,128]{1,0:T(1,128)} %bitcast.1, s32[65]{0:T(128)} %lengths_ref.1), custom_call_target="tpu_custom_call" | custom-call | tf_op jit(solution)/shard_map/pallas_call | solution.py:369
  73.0 0.8 %slice_reduce_fusion = (f32[4,32]{1,0:T(4,128)S(1)}, f32[4,32]{1,0:T(4,128)S(1)}) fusion(f32[4,8,128]{2,1,0:T(8,128)} %shard_map.68), kind=kLoop, calls=%fused_computation | loop fusion | bytes 2048 | tf_op jit(solution)/shard_map/slice | solution.py:427
  73.8 0.6 reshape_squeeze.7
  74.4 0.6 reshape_squeeze.6

commit v14 on v13

--- a/solution.py
+++ b/solution.py
@@ -105,24 +105,31 @@
 
     sends = []
 
-    def send_row(source_z, device, sem_index, from_input):
+    halves = 2
+    half = quarter // halves
+
+    def send_row(source_z, device, sem_index, from_input, parts=range(halves)):
         slot = source_z * c_count + c_index
-        copy = pltpu.make_async_remote_copy(
-            src_ref=normed_out.at[slot],
-            dst_ref=normed_out.at[slot],
-            send_sem=row_send.at[sem_index], recv_sem=row_recv.at[slot],
-            device_id=device, device_id_type=MESH_IDS,
-        )
-        copy.start()
-        sends.append(copy)
-
-    def wait_row(source_z, source_core):
+        for h in parts:
+            rows = pl.ds(h * half, half)
+            copy = pltpu.make_async_remote_copy(
+                src_ref=normed_out.at[slot, rows],
+                dst_ref=normed_out.at[slot, rows],
+                send_sem=row_send.at[sem_index * halves + h], recv_sem=row_recv.at[slot, h],
+                device_id=device, device_id_type=MESH_IDS,
+            )
+            copy.start()
+            sends.append(copy)
+
+    def wait_row(source_z, source_core, parts=range(halves)):
         slot = source_z * c_count + source_core
-        pltpu.make_async_remote_copy(
-            src_ref=normed_out.at[slot], dst_ref=normed_out.at[slot],
-            send_sem=row_send.at[0], recv_sem=row_recv.at[slot],
-            device_id=(x_index, y_index, z_index, other_core), device_id_type=MESH_IDS,
-        ).wait_recv()
+        for h in parts:
+            rows = pl.ds(h * half, half)
+            pltpu.make_async_remote_copy(
+                src_ref=normed_out.at[slot, rows], dst_ref=normed_out.at[slot, rows],
+                send_sem=row_send.at[0], recv_sem=row_recv.at[slot, h],
+                device_id=(x_index, y_index, z_index, other_core), device_id_type=MESH_IDS,
+            ).wait_recv()
 
     right = (x_index, y_index, ring_z(1), c_index)
     left = (x_index, y_index, ring_z(-1), c_index)
@@ -186,16 +193,22 @@
 
     for step in range(1, right_steps + 1):
         from_left = ring_z(-step)
-        wait_row(from_left, c_index)
-        if step < right_steps:
-            send_row(from_left, right, next_sem(), False)
-        send_row(from_left, partner, next_sem(), False)
+        onward = next_sem() if step < right_steps else None
+        across = next_sem()
+        for h in range(halves):
+            wait_row(from_left, c_index, (h,))
+            if onward is not None:
+                send_row(from_left, right, onward, False, (h,))
+            send_row(from_left, partner, across, False, (h,))
         if step <= left_steps:
             from_right = ring_z(step)
-            wait_row(from_right, c_index)
-            if step < left_steps:
-                send_row(from_right, left, next_sem(), False)
-            send_row(from_right, partner, next_sem(), False)
+            onward = next_sem() if step < left_steps else None
+            across = next_sem()
+            for h in range(halves):
+                wait_row(from_right, c_index, (h,))
+                if onward is not None:
+                    send_row(from_right, left, onward, False, (h,))
+                send_row(from_right, partner, across, False, (h,))
 
     for copy in own:
         copy.wait()
@@ -386,8 +399,8 @@
             pltpu.SemaphoreType.DMA((x_count,)),
             pltpu.SemaphoreType.DMA((x_count - 1,)),
             pltpu.SemaphoreType.DMA((x_count,)),
-            pltpu.SemaphoreType.DMA((row_group - 1,)),
-            pltpu.SemaphoreType.DMA((row_group,)),
+            pltpu.SemaphoreType.DMA(((row_group - 1) * 2,)),
+            pltpu.SemaphoreType.DMA((row_group, 2)),
             pltpu.SemaphoreType.DMA((weight_group - 1,)),
             pltpu.SemaphoreType.DMA((weight_group,)),
             pltpu.SemaphoreType.DMA((row_group - 1,)),

time: 75.3 us -> 74.2 us (0.985)
  Pallas kernels: 72.4 us -> 71.3 us
    pallas_call x1, Pallas kernels: 72.4 us -> 71.3 us  [score_all(): pl.pallas_call(functools.partial(fused_kernel, vocab_local), out_shape=ja...]
where the time goes in v14:
time: 74.2 us; the launch traced here: 73.9 us
  Pallas kernels  71.3 us (96%)
  local copies, waits for them, and re-layouts  2 us (3%)
    pallas_call x1, Pallas kernels, score_all(): pl.pallas_call(functools.partial(fused_kernel, vocab_local), out_shape=ja...  71.3 us

profile of v14, /device:TPU:400, one launch (start us, length us, event | category | flops | bytes accessed | tf_op | source)
XLA Modules:
  0.0 73.9 jit_solution(11203112457192508348)
XLA Ops:
  0.6 71.3 %shard_map.68 = f32[4,8,128]{2,1,0:T(8,128)} custom-call(bf16[128,256]{1,0:T(8,128)(2,1)} %hidden_ref.1, bf16[256]{0:T(256)(128)(2,1)} %gain_ref.1, bf16[256,251]{1,0:T(8,128)(2,1)} %weight_ref.1, s32[1,128]{1,0:T(1,128)} %bitcast.1, s32[65]{0:T(128)} %lengths_ref.1), custom_call_target="tpu_custom_call" | custom-call | tf_op jit(solution)/shard_map/pallas_call | solution.py:382
  71.9 0.8 %slice_reduce_fusion = (f32[4,32]{1,0:T(4,128)S(1)}, f32[4,32]{1,0:T(4,128)S(1)}) fusion(f32[4,8,128]{2,1,0:T(8,128)} %shard_map.68), kind=kLoop, calls=%fused_computation | loop fusion | bytes 2048 | tf_op jit(solution)/shard_map/slice | solution.py:440
  72.7 0.6 reshape_squeeze.7
  73.3 0.6 reshape_squeeze.6

commit v15 on v14

--- a/solution.py
+++ b/solution.py
@@ -105,7 +105,7 @@
 
     sends = []
 
-    halves = 2
+    halves = 4
     half = quarter // halves
 
     def send_row(source_z, device, sem_index, from_input, parts=range(halves)):
@@ -399,8 +399,8 @@
             pltpu.SemaphoreType.DMA((x_count,)),
             pltpu.SemaphoreType.DMA((x_count - 1,)),
             pltpu.SemaphoreType.DMA((x_count,)),
-            pltpu.SemaphoreType.DMA(((row_group - 1) * 2,)),
-            pltpu.SemaphoreType.DMA((row_group, 2)),
+            pltpu.SemaphoreType.DMA(((row_group - 1) * 4,)),
+            pltpu.SemaphoreType.DMA((row_group, 4)),
             pltpu.SemaphoreType.DMA((weight_group - 1,)),
             pltpu.SemaphoreType.DMA((weight_group,)),
             pltpu.SemaphoreType.DMA((row_group - 1,)),

time: 74.2 us -> 73.9 us (level)
  the two profiles are of different devices: /device:TPU:400 before, /device:TPU:24 now
where the time goes in v15:
time: 73.9 us; the launch traced here: 73.5 us
  Pallas kernels  70.8 us (96%)
  local copies, waits for them, and re-layouts  2 us (3%)
    pallas_call x1, Pallas kernels, score_all(): pl.pallas_call(functools.partial(fused_kernel, vocab_local), out_shape=ja...  70.8 us

profile of v15, /device:TPU:24, one launch (start us, length us, event | category | flops | bytes accessed | tf_op | source)
XLA Modules:
  0.0 73.5 jit_solution(11797038172421845366)
XLA Ops:
  0.6 70.8 %shard_map.68 = f32[4,8,128]{2,1,0:T(8,128)} custom-call(bf16[128,256]{1,0:T(8,128)(2,1)} %hidden_ref.1, bf16[256]{0:T(256)(128)(2,1)} %gain_ref.1, bf16[256,251]{1,0:T(8,128)(2,1)} %weight_ref.1, s32[1,128]{1,0:T(1,128)} %bitcast.1, s32[65]{0:T(128)} %lengths_ref.1), custom_call_target="tpu_custom_call" | custom-call | tf_op jit(solution)/shard_map/pallas_call | solution.py:382
  71.5 0.8 %slice_reduce_fusion = (f32[4,32]{1,0:T(4,128)S(1)}, f32[4,32]{1,0:T(4,128)S(1)}) fusion(f32[4,8,128]{2,1,0:T(8,128)} %shard_map.68), kind=kLoop, calls=%fused_computation | loop fusion | bytes 2048 | tf_op jit(solution)/shard_map/slice | solution.py:440
  72.3 0.6 reshape_squeeze.7
  72.9 0.6 reshape_squeeze.6

commit v16 on v15

--- a/solution.py
+++ b/solution.py
@@ -142,15 +142,6 @@
         sem_count[0] += 1
         return sem_count[0] - 1
 
-    for step in range(1, weight_group):
-        _, device = weight_peer(step)
-        copy = pltpu.make_async_remote_copy(
-            src_ref=weight_ref, dst_ref=weight_out.at[weight_rank],
-            send_sem=weight_send.at[step - 1], recv_sem=weight_recv.at[weight_rank],
-            device_id=device, device_id_type=MESH_IDS,
-        )
-        copy.start()
-        sends.append(copy)
     for step in range(1, row_group):
         copy = pltpu.make_async_remote_copy(
             src_ref=ids_ref, dst_ref=ids_out.at[row_rank],
@@ -190,6 +181,16 @@
     if left_steps > 0:
         send_row(z_index, left, next_sem(), True)
     send_row(z_index, partner, next_sem(), True)
+
+    for step in range(1, weight_group):
+        _, device = weight_peer(step)
+        copy = pltpu.make_async_remote_copy(
+            src_ref=weight_ref, dst_ref=weight_out.at[weight_rank],
+            send_sem=weight_send.at[step - 1], recv_sem=weight_recv.at[weight_rank],
+            device_id=device, device_id_type=MESH_IDS,
+        )
+        copy.start()
+        sends.append(copy)
 
     for step in range(1, right_steps + 1):
         from_left = ring_z(-step)

time: 73.9 us -> 76 us (1.028)
  Pallas kernels: 70.8 us -> 73.1 us
    pallas_call x1, Pallas kernels: 70.8 us -> 73.1 us  [score_all(): pl.pallas_call(functools.partial(fused_kernel, vocab_local), out_shape=ja...]
where the time goes in v16:
time: 76 us; the launch traced here: 75.7 us
  Pallas kernels  73.1 us (96%)
  local copies, waits for them, and re-layouts  2 us (3%)
    pallas_call x1, Pallas kernels, score_all(): pl.pallas_call(functools.partial(fused_kernel, vocab_local), out_shape=ja...  73.1 us

profile of v16, /device:TPU:24, one launch (start us, length us, event | category | flops | bytes accessed | tf_op | source)
XLA Modules:
  0.0 75.7 jit_solution(10455959295302769258)
XLA Ops:
  0.6 73.1 %shard_map.68 = f32[4,8,128]{2,1,0:T(8,128)} custom-call(bf16[128,256]{1,0:T(8,128)(2,1)} %hidden_ref.1, bf16[256]{0:T(256)(128)(2,1)} %gain_ref.1, bf16[256,251]{1,0:T(8,128)(2,1)} %weight_ref.1, s32[1,128]{1,0:T(1,128)} %bitcast.1, s32[65]{0:T(128)} %lengths_ref.1), custom_call_target="tpu_custom_call" | custom-call | tf_op jit(solution)/shard_map/pallas_call | solution.py:383
  73.7 0.8 %slice_reduce_fusion = (f32[4,32]{1,0:T(4,128)S(1)}, f32[4,32]{1,0:T(4,128)S(1)}) fusion(f32[4,8,128]{2,1,0:T(8,128)} %shard_map.68), kind=kLoop, calls=%fused_computation | loop fusion | bytes 2048 | tf_op jit(solution)/shard_map/slice | solution.py:441
  74.5 0.6 reshape_squeeze.7
  75.1 0.6 reshape_squeeze.6
